TPU v7x, 512 devices: a whole 4x4x16 slice. The times are simulated.
512 devices in a mesh: modes: 64 (over z_lo, x, core), rad: 8 (over z_hi, y).
Axes of the slice: x: 4, y: 4, z: 16 (z_hi: 2, z_lo: 8; z = z_hi * 8 + z_lo), core: 2. Of those that a mesh axis runs over, the one named last changes fastest.
Arguments:
- forcing: bfloat16 [3, 1024, 256, 256], P(None, 'modes', 'rad'), may hold values from -6 to 6
- diffusion: float32 [3], replicated, may hold values from 0.05 to 1
- axial_forward: float32 [256, 256], replicated, may hold values from -0.375 to 0.375
- axial_inverse_map: float32 [256, 256], replicated, may hold values from -0.375 to 0.375
- axial_eigenvalues: float32 [256], replicated, may hold values from 0.05 to 10
- radial_forward: float32 [512, 256, 256], P(('modes', 'rad')), may hold values from -0.375 to 0.375
- radial_backward: float32 [512, 256, 256], P(('modes', 'rad')), may hold values from -0.375 to 0.375
- radial_eigenvalues: float32 [512, 256], P(('modes', 'rad')), may hold values from 0.05 to 10
Outputs:
- solution: float32 [3, 512, 2, 256, 256], P(None, 'modes', None, 'rad')
All inputs are finite; a program needn't handle non-finite values.
Results may differ from a plain program's by a relative error of at most 0.0003.
Values may be sent and summed in bfloat16 or wider, within the bound.
A program may use at most 64 MiB of HBM per device.

v0:
```python
import math

import jax
import jax.numpy as jnp
from jax import lax
from jax.sharding import PartitionSpec as P


def azimuthal_tables(retained, points):
    row_index = jnp.arange(2 * retained, dtype=jnp.int32)
    wavenumber = row_index // 2
    quarter = (row_index % 2).astype(jnp.float32) * (0.5 * math.pi)
    theta_index = jnp.arange(points, dtype=jnp.int32)
    phase_index = wavenumber[:, None] * theta_index[None, :] % points
    radians = phase_index.astype(jnp.float32) * (2.0 * math.pi / points) + quarter[:, None]
    table = jnp.cos(radians) * (1.0 / math.sqrt(points))
    upper = table.astype(jnp.bfloat16)
    widened = lax.optimization_barrier(upper).astype(jnp.float32)
    lower = (table - widened).astype(jnp.bfloat16)
    return (upper, lower)


def modal_solve(spectral_coefficients, forward_map, backward, eigenvalues, axial_part, diffusion):
    highest_mode = lax.Precision.HIGHEST
    radial_coefficients = jnp.einsum(
        "hzv,bhtvp->bhtzp", forward_map, spectral_coefficients, precision=highest_mode
    )
    denominator = 1.0 + diffusion[:, None, None, None, None] * (
        eigenvalues[None, :, None, :, None] + axial_part[None, None, None, None, :]
    )
    return jnp.einsum(
        "mri,fmciq->fmcrq", backward, radial_coefficients / denominator, precision=highest_mode
    )


def per_device(
    forcing,
    diffusion,
    axial_forward,
    axial_inverse_map,
    axial_eigenvalues,
    radial_forward,
    radial_backward,
    radial_eigenvalues,
):
    highest_mode = lax.Precision.HIGHEST
    fields, slab_points, radial_block, axial_points = forcing.shape
    mode_processors = lax.axis_size("modes")
    radial_devices = lax.axis_size("rad")
    total_theta = slab_points * mode_processors
    retained = radial_forward.shape[0] * mode_processors * radial_devices
    table_upper, table_lower = azimuthal_tables(retained, total_theta)
    flat_values = forcing.reshape(fields, slab_points, radial_block * axial_points)
    columns = lax.all_to_all(flat_values, "modes", split_axis=2, concat_axis=1, tiled=True)
    first = jnp.einsum("kt,ftc->fkc", table_upper, columns, preferred_element_type=jnp.float32)
    second = jnp.einsum("kt,ftc->fkc", table_lower, columns, preferred_element_type=jnp.float32)
    spectral = lax.all_to_all(first + second, "modes", split_axis=1, concat_axis=2, tiled=True)
    local_modes = spectral.shape[1] // 2
    spectral = spectral.reshape(fields, local_modes, 2, radial_block, axial_points)
    axial_coef = jnp.einsum("fmcrz,qz->fmcrq", spectral, axial_forward, precision=highest_mode)
    exchanged = lax.all_to_all(axial_coef, "rad", split_axis=4, concat_axis=3, tiled=True)
    forward_rows, backward_rows, eigen_rows = (
        lax.all_gather(radial_forward, "rad", axis=0, tiled=True),
        lax.all_gather(radial_backward, "rad", axis=0, tiled=True),
        lax.all_gather(radial_eigenvalues, "rad", axis=0, tiled=True),
    )
    axial_block = axial_points // radial_devices
    axial_part = lax.dynamic_slice_in_dim(
        axial_eigenvalues, lax.axis_index("rad") * axial_block, axial_block
    )
    solved = modal_solve(exchanged, forward_rows, backward_rows, eigen_rows, axial_part, diffusion)
    returned = lax.all_to_all(solved, "rad", split_axis=3, concat_axis=4, tiled=True)
    return jnp.einsum("fmcrq,zq->fmcrz", returned, axial_inverse_map, precision=highest_mode)


def solution(mesh):
    in_specs = (
        P(None, "modes", "rad", None),
        P(),
        P(),
        P(),
        P(),
        P(("modes", "rad"), None, None),
        P(("modes", "rad"), None, None),
        P(("modes", "rad"), None),
    )
    out_specs = P(None, "modes", None, "rad", None)
    return jax.shard_map(
        per_device, mesh=mesh, in_specs=in_specs, out_specs=out_specs, check_vma=False
    )
```

profile of v0, /device:TPU:192, one launch (start us, length us, event | category | flops | bytes accessed | tf_op | source)
XLA Modules:
  0.0 644.2 jit_solution(5120974905182818223)
XLA Ops:
  6.5 0.0 copy-start
  6.5 9.0 %copy.15 = bf16[3,16,32,256]{1,0,3,2:T(4,128)(2,1)} copy(bf16[3,16,32,256]{3,2,1,0:T(8,128)(2,1)} %param.8) | data formatting | bytes 1572864 | tf_op args[0]
  15.5 13.8 %reshape.58 = bf16[64,2,3072]{2,1,0:T(2,128)(2,1)} reshape(bf16[8192,3,16]{2,1,0:T(4,128)(2,1)} %bitcast.80) | data formatting | bytes 1572864
  29.3 13.6 %all-to-all-start = ((bf16[64,2,3072]{2,1,0:T(2,128)(2,1)}), bf16[64,2,3072]{2,1,0:T(2,128)(2,1)S(1)}, u32[]{:S(2)}, u32[]{:S(2)}) async-start(bf16[64,2,3072]{2,1,0:T(2,128)(2,1)} %reshape.58), calls=%async_computation | async-start | bytes 1572864 | tf_op jit(solution)/shard_map/all_to_all | solution.py:54
  42.9 17.4 %fusion.19 = bf16[1024,1024]{1,0:T(8,128)(2,1)S(1)} fusion(f32[1024]{0:T(1024)S(1)} %fusion.39, s32[1024]{0:T(1024)S(1)} %add_select_fusion.1), kind=kLoop, calls=%fused_computation.23 | loop fusion | flops 17825792 | bytes 2105344 | tf_op jit(solution)/shard_map/convert_element_type | solution.py:17
  60.3 19.5 %all-to-all-done = bf16[64,2,3072]{2,1,0:T(2,128)(2,1)S(1)} async-done(((bf16[64,2,3072]{2,1,0:T(2,128)(2,1)}), bf16[64,2,3072]{2,1,0:T(2,128)(2,1)S(1)}, u32[]{:S(2)}, u32[]{:S(2)}) %all-to-all-start) | async-done | bytes 786464 | tf_op jit(solution)/shard_map/all_to_all | solution.py:54
  79.8 10.8 %reshape.59 = bf16[8192,3,16]{2,1,0:T(4,128)(2,1)} reshape(bf16[64,2,3072]{2,1,0:T(2,128)(2,1)S(1)} %all-to-all-done) | data formatting | bytes 1572864
  90.6 9.7 %copy.30 = bf16[3,16,64,128]{3,1,2,0:T(8,128)(2,1)S(1)} copy(bf16[3,16,64,128]{1,0,3,2:T(4,128)(2,1)} %bitcast.79) | data formatting | bytes 1572864 | tf_op jit(solution)/shard_map/all_to_all | solution.py:54
  100.3 22.6 %fusion.10 = f32[1024,3,128]{2,0,1:T(8,128)S(1)} fusion(bf16[3,1024,128]{2,1,0:T(8,128)(2,1)S(1)} %bitcast.89, bf16[1024,1024]{1,0:T(8,128)(2,1)S(1)} %fusion.19, f32[1024]{0:T(1024)S(1)} %fusion.39, s32[1024]{0:T(1024)S(1)} %add_select_fusion.1), kind=kOutput, calls=%fused_computation.16 | convolution fusion | flops 825229312 | bytes 4464640 | tf_op jit(solution)/shard_map/kt,ftc->fkc/dot_general | solution.py:56
  122.9 22.4 %add_bitcast_fusion = f32[3,1024,128]{2,1,0:T(8,128)S(1)} fusion(f32[1024,3,128]{2,0,1:T(8,128)S(1)} %fusion.10, bf16[3,1024,128]{2,1,0:T(8,128)(2,1)S(1)} %bitcast.90, f32[1024]{0:T(1024)S(1)} %fusion.39, s32[1024]{0:T(1024)S(1)} %add_select_fusion.1), kind=kOutput, calls=%fused_computation.27 | convolution fusion | flops 823525376 | bytes 3940352 | tf_op jit(solution)/shard_map/kt,ftc->fkc/dot_general | solution.py:55
  145.4 2.4 copy.18
  147.8 11.1 %all-to-all-start.1 = ((f32[3,1024,128]{2,0,1:T(4,128)}), f32[3,1024,128]{2,0,1:T(4,128)S(1)}, u32[]{:S(2)}, u32[]{:S(2)}) async-start(f32[3,1024,128]{2,0,1:T(4,128)} %copy.18), calls=%async_computation.1 | async-start | bytes 4194304 | tf_op jit(solution)/shard_map/all_to_all | solution.py:57
  158.9 0.0 all-gather.4.cloned.1.call-start
  159.0 0.7 all-gather.4.cloned.1.call-update
  159.7 148.0 %all-to-all-done.1 = f32[3,1024,128]{2,0,1:T(4,128)S(1)} async-done(((f32[3,1024,128]{2,0,1:T(4,128)}), f32[3,1024,128]{2,0,1:T(4,128)S(1)}, u32[]{:S(2)}, u32[]{:S(2)}) %all-to-all-start.1) | async-done | bytes 1572896 | tf_op jit(solution)/shard_map/all_to_all | solution.py:57
  307.7 2.1 copy.40
  309.7 1.7 reshape.49
  311.4 0.0 copy-done
  311.5 1.4 fusion.30
  312.9 6.8 %copy.20 = f32[3,8,2,32,256]{3,2,1,0,4:T(2,128)} copy(f32[3,8,2,32,256]{4,3,2,1,0:T(8,128)S(1)} %fusion.30) | data formatting | bytes 3145728 | tf_op jit(solution)/shard_map/fmcrz,qz->fmcrq/dot_general | solution.py:60
  319.7 0.0 copy-start.3
  319.7 0.0 copy-start.5
  319.7 0.0 copy-start.4
  319.7 9.6 %reshape.60 = f32[8,1,49152]{2,1,0:T(1,128)} reshape(f32[256,3,8,2,32]{4,3,2,1,0:T(2,128)} %bitcast.85) | data formatting | bytes 3145728
  329.3 10.2 %all-to-all-start.2 = ((f32[8,1,49152]{2,1,0:T(1,128)}), f32[8,1,49152]{2,1,0:T(1,128)S(1)}, u32[]{:S(2)}, u32[]{:S(2)}) async-start(f32[8,1,49152]{2,1,0:T(1,128)} %reshape.60), calls=%async_computation.2 | async-start | bytes 3145728 | tf_op jit(solution)/shard_map/all_to_all | solution.py:61
  339.5 0.0 all-gather.6.cloned.1.call-start
  339.5 0.7 all-gather.6.cloned.1.call-update
  340.2 0.0 copy-done.3
  340.3 65.6 %all-gather = f32[8,1,256]{2,1,0:T(1,128)S(1)} all-gather(f32[1,1,256]{2,1,0:T(1,128)S(1)} %bitcast.92), channel_id=1, replica_groups=mesh['modes'=64,'rad'=8] {'rad'}, dimensions={0}, use_global_device_ids=true | all-gather | bytes 9216 | tf_op jit(solution)/shard_map/all_gather | solution.py:65
  405.8 0.0 copy-done.5
  405.9 0.1 dynamic_slice.3
  405.9 0.1 broadcast_add_fusion
  406.0 0.0 copy-done.4
  406.0 1.0 multiply_add_fusion
  407.1 0.0 all-to-all-done.2
  407.1 0.5 broadcast.102
  407.6 4.4 reduce
  412.0 7.9 %reshape.61 = f32[256,3,8,2,32]{4,3,2,1,0:T(2,128)} reshape(f32[8,49152]{1,0:T(8,128)S(1)} %reduce) | data formatting | bytes 3145728
  419.9 9.3 %copy.39 = f32[3,8,2,32,8,32]{3,4,5,2,1,0:T(8,128)} copy(f32[3,8,2,32,8,32]{3,2,1,0,5,4:T(2,128)} %bitcast.81) | data formatting | bytes 3145728 | tf_op jit(solution)/shard_map/all_to_all | solution.py:61
  429.2 4.3 all_to_all.60
  433.4 0.0 all-gather.4.cloned.1.call-done
  433.5 3.9 fusion.14
  437.4 66.5 %all-gather.6.cloned.1.call-done = f32[8,256,256]{2,1,0:T(8,128)} async-done(((f32[1,256,256]{2,1,0:T(8,128)}), f32[8,256,256]{2,1,0:T(8,128)}) %all-gather.6.cloned.1.call-update) | async-done | bytes 2097168 | tf_op jit(solution)/shard_map/all_gather | solution.py:64
  503.9 4.2 fusion.21
  508.1 6.6 %copy.23 = f32[3,8,2,256,32]{4,2,0,1,3:T(2,128)} copy(f32[3,8,2,256,32]{3,4,2,0,1:T(8,128)S(1)} %fusion.21) | data formatting | bytes 3145728 | tf_op jit(solution)/shard_map/mri,fmciq->fmcrq/transpose | solution.py:31
  514.7 8.7 %reshape.62 = f32[8,1,49152]{2,1,0:T(1,128)S(1)} reshape(f32[256,8,3,2,32]{4,3,2,1,0:T(2,128)} %bitcast.86) | data formatting | bytes 3145728
  523.4 85.0 %all_to_all.69 = f32[8,1,49152]{2,1,0:T(1,128)S(1)} all-to-all(f32[8,1,49152]{2,1,0:T(1,128)S(1)} %reshape.62), channel_id=1, replica_groups=mesh['modes'=64,'rad'=8] {'rad'}, dimensions={0} | all-to-all | bytes 3145728 | tf_op jit(solution)/shard_map/all_to_all | solution.py:72
  608.4 4.4 reduce.1
  612.8 7.9 %reshape.63 = f32[256,8,3,2,32]{4,3,2,1,0:T(2,128)} reshape(f32[8,49152]{1,0:T(8,128)S(1)} %reduce.1) | data formatting | bytes 3145728
  620.7 9.3 %copy.38 = f32[3,8,2,8,32,32]{5,3,4,2,1,0:T(8,128)} copy(f32[3,8,2,8,32,32]{5,2,0,1,4,3:T(2,128)} %bitcast.83) | data formatting | bytes 3145728 | tf_op jit(solution)/shard_map/all_to_all | solution.py:72
  630.0 0.0 copy-start.2
  630.0 0.0 copy-start.1
  630.0 4.3 all_to_all.64
  634.3 0.0 copy-done.2
  634.4 2.6 fusion.28
  636.9 0.0 copy-done.1
  (3 shorter events, 0.0 us)
Async XLA Ops:
  6.5 304.9 %copy-start = (f32[256,256]{1,0:T(8,128)S(1)}, f32[256,256]{1,0:T(8,128)}, u32[]{:S(2)}) copy-start(f32[256,256]{1,0:T(8,128)} %param.10) | copy-start | bytes 786436
  29.3 50.5 %all-to-all-start = ((bf16[64,2,3072]{2,1,0:T(2,128)(2,1)}), bf16[64,2,3072]{2,1,0:T(2,128)(2,1)S(1)}, u32[]{:S(2)}, u32[]{:S(2)}) async-start(bf16[64,2,3072]{2,1,0:T(2,128)(2,1)} %reshape.58), calls=%async_computation | async-start | bytes 1572864 | tf_op jit(solution)/shard_map/all_to_all | solution.py:54
  147.8 159.9 %all-to-all-start.1 = ((f32[3,1024,128]{2,0,1:T(4,128)}), f32[3,1024,128]{2,0,1:T(4,128)S(1)}, u32[]{:S(2)}, u32[]{:S(2)}) async-start(f32[3,1024,128]{2,0,1:T(4,128)} %copy.18), calls=%async_computation.1 | async-start | bytes 4194304 | tf_op jit(solution)/shard_map/all_to_all | solution.py:57
  158.9 274.5 %all-gather.4.cloned.1.call-start = ((), (), s32[]{:S(2)}) async-start(), calls=%async_computation.4 | async-start | bytes 2359296 | tf_op jit(solution)/shard_map/all_gather | solution.py:63
  319.7 20.6 %copy-start.3 = (f32[1,256]{1,0:T(1,128)S(1)}, f32[1,256]{1,0:T(1,128)}, u32[]{:S(2)}) copy-start(f32[1,256]{1,0:T(1,128)} %param.15) | copy-start | bytes 3076
  319.7 86.2 %copy-start.5 = (f32[256]{0:T(256)S(1)}, f32[256]{0:T(256)}, u32[]{:S(2)}) copy-start(f32[256]{0:T(256)} %param.12) | copy-start | bytes 3076
  319.7 86.4 %copy-start.4 = (f32[3]{0:T(128)S(1)}, f32[3]{0:T(128)}, u32[]{:S(2)}) copy-start(f32[3]{0:T(128)} %param.9) | copy-start | bytes 40
  329.3 77.8 %all-to-all-start.2 = ((f32[8,1,49152]{2,1,0:T(1,128)}), f32[8,1,49152]{2,1,0:T(1,128)S(1)}, u32[]{:S(2)}, u32[]{:S(2)}) async-start(f32[8,1,49152]{2,1,0:T(1,128)} %reshape.60), calls=%async_computation.2 | async-start | bytes 3145728 | tf_op jit(solution)/shard_map/all_to_all | solution.py:61
  339.5 164.4 %all-gather.6.cloned.1.call-start = ((), (), s32[]{:S(2)}) async-start(), calls=%async_computation.5 | async-start | bytes 2359296 | tf_op jit(solution)/shard_map/all_gather | solution.py:64
  630.0 4.4 copy-start.2
  630.0 6.9 %copy-start.1 = (f32[256,256]{1,0:T(8,128)S(1)}, f32[256,256]{1,0:T(8,128)}, u32[]{:S(2)}) copy-start(f32[256,256]{1,0:T(8,128)} %param.10) | copy-start | bytes 786436
Sparse Core Ops, SparseCore 0:
  163.0 136.3 all-gather.3
  343.5 160.2 all-gather.5
where the time goes:
time: 654 us; the launch traced here: 644 us
  waiting for transfers between devices  235 us (36%)
  blocking collectives  151 us (23%)
  local copies, waits for them, and re-layouts  125 us (19%)
  matrix products  57.1 us (9%)
  starting transfers between devices  35 us (5%)
  other arithmetic  27.3 us (4%)
  between operations  14 us (2%)
    all_to_all x1, waiting for transfers between devices, per_device(): lax.all_to_all(first + second, 'modes', split_axis=1, concat_axis=2, tile...  148 us
    all_to_all x1, blocking collectives, per_device(): lax.all_to_all(solved, 'rad', split_axis=3, concat_axis=4, tiled=True)  85 us
    unnamed x20, local copies, waits for them, and re-layouts  67.7 us
    all_gather x1, waiting for transfers between devices, per_device(): lax.all_gather(radial_backward, 'rad', axis=0, tiled=True)  66.5 us
    all_gather x1, blocking collectives, per_device(): lax.all_gather(radial_eigenvalues, 'rad', axis=0, tiled=True)  65.6 us
    dot_general x1, matrix products, per_device(): jnp.einsum('kt,ftc->fkc', table_lower, columns, preferred_element_type=jn...  22.6 us
    dot_general x1, matrix products, per_device(): jnp.einsum('kt,ftc->fkc', table_upper, columns, preferred_element_type=jn...  22.4 us
    all_to_all x1, waiting for transfers between devices, per_device(): lax.all_to_all(flat_values, 'modes', split_axis=2, concat_axis=1, tiled=T...  19.5 us
  transfers between devices with their start and end apart: 5, of which 3 were waited for; matrix products, arithmetic and copies ran while one was open for 10% of the time, Pallas kernels for 0%

commit v1 on v0

v1 whole, which is shorter than its diff:
```python
import math

import jax
import jax.numpy as jnp
from jax import lax
from jax.sharding import PartitionSpec as P

GLOBAL = True


def split_table(points, rows):
    k = jnp.arange(rows, dtype=jnp.int32)
    t = jnp.arange(points, dtype=jnp.int32)
    quarter = (k % 2).astype(jnp.float32) * (0.5 * math.pi)
    phase = ((k // 2)[:, None] * t[None, :]) % points
    radians = phase.astype(jnp.float32) * (2.0 * math.pi / points) + quarter[:, None]
    table = jnp.cos(radians) * (1.0 / math.sqrt(points))
    upper = table.astype(jnp.bfloat16)
    widened = lax.optimization_barrier(upper).astype(jnp.float32)
    lower = (table - widened).astype(jnp.bfloat16)
    return upper, lower


def per_device(forcing, diffusion, axial_forward, axial_inverse_map, axial_eigenvalues,
               radial_forward, radial_backward, radial_eigenvalues):
    hi = lax.Precision.HIGHEST
    fields, slab, rblock, nz = forcing.shape
    nm, nrad = lax.axis_size("modes"), lax.axis_size("rad")
    points = slab * nm
    nr = rblock * nrad
    modes = nm * nrad
    cols = rblock * nz // nm
    halves = nz // cols
    up, lo = split_table(points, 2 * modes)
    x = forcing.reshape(fields, slab, rblock, halves, cols)
    x = x.transpose(2, 3, 0, 1, 4).reshape(nm, fields, slab, cols)
    got = lax.all_to_all(x, "modes", split_axis=0, concat_axis=0, tiled=True)
    got = got.transpose(0, 2, 1, 3).reshape(points, fields * cols)
    spec = jnp.dot(up, got, preferred_element_type=jnp.float32) + jnp.dot(
        lo, got, preferred_element_type=jnp.float32)
    if GLOBAL:
        spec = spec.reshape(modes, 2, fields * cols)
        here = lax.all_to_all(spec, ("modes", "rad"), split_axis=0, concat_axis=0, tiled=True)
        here = here.reshape(nm, nrad, 2, fields, cols)
    else:
        spec = spec.reshape(nm, nrad, 2, fields * cols)
        here = lax.all_to_all(spec, "modes", split_axis=0, concat_axis=0, tiled=True)
        here = lax.all_to_all(here, "rad", split_axis=1, concat_axis=1, tiled=True)
        here = here.reshape(nm, nrad, 2, fields, cols)
    here = here.reshape(rblock, halves, nrad, 2, fields, cols)
    here = here.transpose(4, 3, 2, 0, 1, 5).reshape(fields, 2, nr, nz)
    axial = jnp.einsum("fcrz,qz->fcrq", here, axial_forward, precision=hi)
    radial = jnp.einsum("ir,fcrq->fciq", radial_forward[0], axial, precision=hi)
    denominator = 1.0 + diffusion[:, None, None, None] * (
        radial_eigenvalues[0][None, None, :, None] + axial_eigenvalues[None, None, None, :])
    scaled = radial / denominator
    returned = jnp.einsum("ri,fciq->fcrq", radial_backward[0], scaled, precision=hi)
    out = jnp.einsum("zq,fcrq->fcrz", axial_inverse_map, returned, precision=hi)
    out = out.reshape(fields, 1, 2, nr, nz)
    return lax.all_to_all(out, "rad", split_axis=3, concat_axis=1, tiled=True)


def solution(mesh):
    in_specs = (P(None, "modes", "rad", None), P(), P(), P(), P(),
                P(("modes", "rad"), None, None), P(("modes", "rad"), None, None),
                P(("modes", "rad"), None))
    return jax.shard_map(per_device, mesh=mesh, in_specs=in_specs,
                         out_specs=P(None, "modes", None, "rad", None), check_vma=False)
```

time: 654 us -> 295 us (0.45)
  the two profiles are of different devices: /device:TPU:192 before, /device:TPU:32 now
where the time goes in v1:
time: 295 us; the launch traced here: 291 us
  waiting for transfers between devices  97.9 us (33%)
  blocking collectives  82.9 us (28%)
  matrix products  40.3 us (14%)
  starting transfers between devices  34 us (12%)
  other arithmetic  17.8 us (6%)
  local copies, waits for them, and re-layouts  17.7 us (6%)
    all_to_all x1, blocking collectives, per_device(): return lax.all_to_all(out, 'rad', split_axis=3, concat_axis=1, tiled=True)  82.9 us
    all_to_all x1, waiting for transfers between devices, per_device(): lax.all_to_all(spec, ('modes', 'rad'), split_axis=0, concat_axis=0, tiled...  77.6 us
    all_to_all x1, waiting for transfers between devices, per_device(): got = lax.all_to_all(x, 'modes', split_axis=0, concat_axis=0, tiled=True)  20.4 us
    all_to_all x1, starting transfers between devices, per_device(): lax.all_to_all(spec, ('modes', 'rad'), split_axis=0, concat_axis=0, tiled...  18.3 us
    convert_element_type x1, other arithmetic, split_table(): upper = table.astype(jnp.bfloat16)  17.6 us
    dot_general x1, matrix products, per_device(): jnp.dot(lo, got, preferred_element_type=jnp.float32)  16.7 us
    dot_general x1, matrix products, per_device(): jnp.dot(up, got, preferred_element_type=jnp.float32)  16.4 us
    all_to_all x1, starting transfers between devices, per_device(): got = lax.all_to_all(x, 'modes', split_axis=0, concat_axis=0, tiled=True)  15.7 us
  transfers between devices with their start and end apart: 2, of which 2 were waited for; matrix products, arithmetic and copies ran while one was open for 6% of the time, Pallas kernels for 0%

profile of v1, /device:TPU:32, one launch (start us, length us, event | category | flops | bytes accessed | tf_op | source)
XLA Modules:
  0.0 291.1 jit_solution(4464815962577270002)
XLA Ops:
  0.0 0.0 copy-start
  0.0 2.1 reshape.85
  2.1 1.8 copy.14
  3.9 15.7 %all-to-all-start = ((bf16[64,3,16,128]{3,2,1,0:T(8,128)(2,1)}), bf16[64,3,16,128]{3,2,1,0:T(8,128)(2,1)S(1)}, u32[]{:S(2)}, u32[]{:S(2)}) async-start(bf16[64,3,16,128]{3,2,1,0:T(8,128)(2,1)} %bitcast.1), calls=%async_computation | async-start | bytes 1572864 | tf_op jit(solution)/shard_map/all_to_all | solution.py:37
  19.5 17.6 %fusion.11 = bf16[1024,1024]{1,0:T(8,128)(2,1)S(1)} fusion(f32[1024]{0:T(1024)S(1)} %fusion.37, s32[1024]{0:T(1024)S(1)} %add_select_fusion.1), kind=kLoop, calls=%fused_computation.14 | loop fusion | flops 17825792 | bytes 2105344 | tf_op jit(solution)/shard_map/convert_element_type | solution.py:18
  37.1 20.4 %all-to-all-done = bf16[64,3,16,128]{3,2,1,0:T(8,128)(2,1)S(1)} async-done(((bf16[64,3,16,128]{3,2,1,0:T(8,128)(2,1)}), bf16[64,3,16,128]{3,2,1,0:T(8,128)(2,1)S(1)}, u32[]{:S(2)}, u32[]{:S(2)}) %all-to-all-start) | async-done | bytes 786464 | tf_op jit(solution)/shard_map/all_to_all | solution.py:37
  57.5 0.5 copy.15
  58.0 16.7 %fusion.9 = f32[1024,384]{1,0:T(8,128)S(1)} fusion(bf16[1024,1024]{1,0:T(8,128)(2,1)S(1)} %fusion.11, f32[1024]{0:T(1024)S(1)} %fusion.37, s32[1024]{0:T(1024)S(1)} %add_select_fusion.1, bf16[128,8,3,128]{3,2,1,0:T(4,128)(2,1)S(1)} %bitcast.62), kind=kOutput, calls=%fused_computation.13 | convolution fusion | flops 825229312 | bytes 4464640 | tf_op jit(solution)/shard_map/dot_general | solution.py:39
  74.8 16.4 %convolution_add_fusion = f32[1024,384]{1,0:T(8,128)S(1)} fusion(f32[1024,384]{1,0:T(8,128)S(1)} %fusion.9, bf16[128,8,3,128]{3,2,1,0:T(4,128)(2,1)S(1)} %bitcast.63, f32[1024]{0:T(1024)S(1)} %fusion.37, s32[1024]{0:T(1024)S(1)} %add_select_fusion.1), kind=kOutput, calls=%fused_computation.21 | convolution fusion | flops 823525376 | bytes 3940352 | tf_op jit(solution)/shard_map/dot_general | solution.py:39
  91.1 2.1 reshape.88
  93.2 0.0 copy-start.3
  93.2 0.0 copy-start.4
  93.2 0.0 copy-start.5
  93.2 18.3 %all-to-all-start.1 = ((f32[512,2,384]{2,1,0:T(2,128)}), f32[512,2,384]{2,1,0:T(2,128)S(1)}, u32[]{:S(2)}, u32[]{:S(2)}) async-start(f32[512,2,384]{2,1,0:T(2,128)} %reshape.88), calls=%async_computation.1 | async-start | bytes 3145728 | tf_op jit(solution)/shard_map/all_to_all | solution.py:43
  111.5 0.0 copy-done.3
  111.5 0.0 copy-done.4
  111.6 0.1 broadcast_add_fusion
  111.7 0.0 copy-done.5
  111.7 0.1 multiply_add_fusion
  111.8 77.6 %all-to-all-done.1 = f32[512,2,384]{2,1,0:T(2,128)S(1)} async-done(((f32[512,2,384]{2,1,0:T(2,128)}), f32[512,2,384]{2,1,0:T(2,128)S(1)}, u32[]{:S(2)}, u32[]{:S(2)}) %all-to-all-start.1) | async-done | bytes 1572896 | tf_op jit(solution)/shard_map/all_to_all | solution.py:43
  189.4 1.2 copy.16
  190.6 2.5 reshape_reshape.3
  193.1 2.4 copy.17
  195.5 2.5 reshape.89
  198.0 0.0 copy-done
  198.0 0.0 copy-start.1
  198.0 1.6 fusion.28
  199.6 0.0 copy-done.1
  199.6 0.0 copy-start.6
  199.6 1.5 fusion.26
  201.1 0.0 copy-done.6
  201.1 0.0 copy-start.2
  201.1 1.5 fusion.14
  202.6 0.0 copy-done.2
  202.6 2.8 fusion.15
  205.4 1.2 copy.20
  206.6 82.9 %all_to_all.28 = f32[3,1,2,256,256]{4,2,0,1,3:T(2,128)S(1)} all-to-all(f32[3,1,2,256,256]{4,2,0,1,3:T(2,128)S(1)} %copy.20), channel_id=1, replica_groups=mesh['modes'=64,'rad'=8] {'rad'}, dimensions={3} | all-to-all | bytes 3145728 | tf_op jit(solution)/shard_map/all_to_all | solution.py:60
  289.5 1.4 copy.38
  (2 shorter events, 0.0 us)
Async XLA Ops:
  0.0 198.0 %copy-start = (f32[256,256]{1,0:T(8,128)S(1)}, f32[256,256]{1,0:T(8,128)}, u32[]{:S(2)}) copy-start(f32[256,256]{1,0:T(8,128)} %param.10) | copy-start | bytes 786436
  3.9 53.6 %all-to-all-start = ((bf16[64,3,16,128]{3,2,1,0:T(8,128)(2,1)}), bf16[64,3,16,128]{3,2,1,0:T(8,128)(2,1)S(1)}, u32[]{:S(2)}, u32[]{:S(2)}) async-start(bf16[64,3,16,128]{3,2,1,0:T(8,128)(2,1)} %bitcast.1), calls=%async_computation | async-start | bytes 1572864 | tf_op jit(solution)/shard_map/all_to_all | solution.py:37
  93.2 18.3 %copy-start.3 = (f32[256]{0:T(256)S(1)}, f32[256]{0:T(256)}, u32[]{:S(2)}) copy-start(f32[256]{0:T(256)} %param.12) | copy-start | bytes 3076
  93.2 18.4 %copy-start.4 = (f32[1,256]{1,0:T(1,128)S(1)}, f32[1,256]{1,0:T(1,128)}, u32[]{:S(2)}) copy-start(f32[1,256]{1,0:T(1,128)} %param.15) | copy-start | bytes 3076
  93.2 18.5 %copy-start.5 = (f32[3]{0:T(128)S(1)}, f32[3]{0:T(128)}, u32[]{:S(2)}) copy-start(f32[3]{0:T(128)} %param.9) | copy-start | bytes 40
  93.2 96.2 %all-to-all-start.1 = ((f32[512,2,384]{2,1,0:T(2,128)}), f32[512,2,384]{2,1,0:T(2,128)S(1)}, u32[]{:S(2)}, u32[]{:S(2)}) async-start(f32[512,2,384]{2,1,0:T(2,128)} %reshape.88), calls=%async_computation.1 | async-start | bytes 3145728 | tf_op jit(solution)/shard_map/all_to_all | solution.py:43
  198.0 1.6 copy-start.1
  199.6 1.5 copy-start.6
  201.1 1.5 copy-start.2

commit v2 on v1

v2 whole, which is shorter than its diff:
```python
import functools
import math

import jax
import jax.numpy as jnp
from jax import lax
from jax.experimental import pallas as pl
from jax.experimental.pallas import tpu as pltpu
from jax.sharding import PartitionSpec as P

F32, BF16 = jnp.float32, jnp.bfloat16
SPECTRUM_OCTAVES, SOLVED_OCTAVES = 16, 10


def encode(x, inverse_floor, octaves):
    grown = jnp.log2(1.0 + jnp.abs(x) * inverse_floor)
    code = jnp.exp2(grown * (239.0 / octaves) - 120.0)
    return jnp.where(x < 0, -code, code).astype(BF16)


def decode(code, floor, octaves):
    code = code.astype(F32)
    grown = (jnp.log2(jnp.abs(code)) + 120.0) * (octaves / 239.0)
    size = (jnp.exp2(grown) - 1.0) * floor
    return jnp.where(code < 0, -size, size)


def split(x):
    high = x.astype(BF16)
    return high, (x - high.astype(F32)).astype(BF16)


def dot3(a, b, dims):
    d = functools.partial(lax.dot_general, dimension_numbers=(dims, ((), ())), preferred_element_type=F32)
    return d(a[0], b[0]) + (d(a[0], b[1]) + d(a[1], b[0]))


NN, NT_ = ((1,), (0,)), ((1,), (1,))


def azimuthal_tables(points, rows):
    step = 32
    t = jnp.arange(points, dtype=jnp.int32)
    turn = 2.0 * math.pi / points

    def angles(k):
        return ((k[:, None] * t[None, :]) % points).astype(F32) * turn

    coarse = angles(step * jnp.arange(rows // 2 // step, dtype=jnp.int32))
    fine = angles(jnp.arange(step, dtype=jnp.int32))
    scale = 1.0 / math.sqrt(points)
    ca, sa, cb, sb = lax.optimization_barrier(
        (jnp.cos(coarse), jnp.sin(coarse), jnp.cos(fine) * scale, jnp.sin(fine) * scale))
    ca, sa = ca[:, None], sa[:, None]
    real = ca * cb[None] - sa * sb[None]
    imag = -(sa * cb[None] + ca * sb[None])
    table = jnp.stack([real, imag], axis=2).reshape(rows, points)
    upper = table.astype(BF16)
    lower = (table - lax.optimization_barrier(upper).astype(F32)).astype(BF16)
    return upper, lower


def transform_kernel(up_ref, lo_ref, got_ref, bound_ref, out_ref):
    fields = got_ref.shape[1]
    points, cols = got_ref.shape[0] * got_ref.shape[2], got_ref.shape[3]
    inverse_floor = 2.0 ** (SPECTRUM_OCTAVES - 5) / bound_ref[0:1, :]
    for f in range(fields):
        data = got_ref[:, f].reshape(points, cols)
        spec = jnp.dot(up_ref[...], data, preferred_element_type=F32) + jnp.dot(
            lo_ref[...], data, preferred_element_type=F32)
        out_ref[f] = encode(spec, inverse_floor, SPECTRUM_OCTAVES)


def transform(up, lo, got, bound):
    rows, points = up.shape
    fields, cols = got.shape[1], got.shape[3]
    block = rows // 4
    return pl.pallas_call(
        transform_kernel,
        grid=(rows // block,),
        in_specs=[pl.BlockSpec((block, points), lambda i: (i, 0)),
                  pl.BlockSpec((block, points), lambda i: (i, 0)),
                  pl.BlockSpec(got.shape, lambda i: (0, 0, 0, 0)),
                  pl.BlockSpec(bound.shape, lambda i: (0, 0))],
        out_specs=pl.BlockSpec((fields, block, cols), lambda i: (0, i, 0)),
        out_shape=jax.ShapeDtypeStruct((fields, rows, cols), BF16),
        compiler_params=pltpu.CompilerParams(vmem_limit_bytes=48 << 20),
    )(up, lo, got, bound)


def solve_kernel(rblock, nrad, codes_ref, bound_ref, diff_ref, af_ref, ai_ref, qeig_ref, rf_ref, rb_ref, reig_ref,
                 out_ref, dec, x):
    f = pl.program_id(0)
    nr, nz = x.shape[1], x.shape[2]
    cols = codes_ref.shape[2]
    halves = nz // cols
    stride = halves * nrad * 2
    floor = bound_ref[0:1, :] * 2.0 ** (5 - SPECTRUM_OCTAVES)
    dec[...] = decode(codes_ref[0], floor, SPECTRUM_OCTAVES)
    for c in range(2):
        for s in range(nrad):
            for h in range(halves):
                x[c, s * rblock:(s + 1) * rblock, h * cols:(h + 1) * cols] = dec[
                    pl.ds(h * nrad * 2 + s * 2 + c, rblock, stride=stride), :]
    af, ai = split(af_ref[...]), split(ai_ref[...])
    rf, rb = split(rf_ref[0]), split(rb_ref[0])
    axial = dot3(split(x[...].reshape(2 * nr, nz)), af, NT_)
    inverse = 1.0 + diff_ref[f] * (reig_ref[...] + qeig_ref[...])
    returned = []
    for c in range(2):
        scaled = dot3(rf, split(axial[c * nr:(c + 1) * nr]), NN) / inverse
        returned.append(dot3(rb, split(scaled), NN))
    out = [dot3(split(r), ai, NT_) for r in returned]
    top = jnp.maximum(jnp.max(jnp.abs(out[0]), axis=0, keepdims=True), jnp.max(jnp.abs(out[1]), axis=0, keepdims=True))
    top = jnp.broadcast_to(jnp.max(top, axis=1, keepdims=True), (16, nz))
    top = (jnp.maximum(top, 1e-30) * 1.01).astype(BF16)
    inverse_floor = 2.0 ** SOLVED_OCTAVES / top[0:1].astype(F32)
    for c in range(2):
        code = encode(out[c], inverse_floor, SOLVED_OCTAVES)
        for s in range(nrad):
            out_ref[s, 0, c * rblock:(c + 1) * rblock, :] = code[s * rblock:(s + 1) * rblock]
    for s in range(nrad):
        out_ref[s, 0, 2 * rblock:, :] = top


def solve(codes, bound, diffusion, af, ai, qeig, rf, rb, reig, rblock, nrad):
    fields, rows, cols = codes.shape
    nr, nz = rblock * nrad, af.shape[0]

    def whole(a):
        return pl.BlockSpec(a.shape, lambda f: (0,) * a.ndim)

    return pl.pallas_call(
        functools.partial(solve_kernel, rblock, nrad),
        grid=(fields,),
        in_specs=[pl.BlockSpec((1, rows, cols), lambda f: (f, 0, 0)), whole(bound),
                  pl.BlockSpec(memory_space=pltpu.SMEM), whole(af), whole(ai), whole(qeig), whole(rf), whole(rb),
                  whole(reig)],
        out_specs=pl.BlockSpec((nrad, 1, 2 * rblock + 16, nz), lambda f: (0, f, 0, 0)),
        out_shape=jax.ShapeDtypeStruct((nrad, fields, 2 * rblock + 16, nz), BF16),
        scratch_shapes=[pltpu.VMEM((rows, cols), F32), pltpu.VMEM((2, nr, nz), F32)],
        compiler_params=pltpu.CompilerParams(vmem_limit_bytes=48 << 20),
    )(codes, bound, diffusion, af, ai, qeig, rf, rb, reig)


def unpack_kernel(rblock, codes_ref, out_ref):
    for f in range(codes_ref.shape[1]):
        floor = codes_ref[0, f, 2 * rblock:2 * rblock + 1, :].astype(F32) * 2.0 ** -SOLVED_OCTAVES
        for c in range(2):
            out_ref[f, 0, c] = decode(codes_ref[0, f, c * rblock:(c + 1) * rblock, :], floor, SOLVED_OCTAVES)


def unpack(codes, rblock):
    nrad, fields, rows, nz = codes.shape
    return pl.pallas_call(
        functools.partial(unpack_kernel, rblock),
        grid=(nrad,),
        in_specs=[pl.BlockSpec((1, fields, rows, nz), lambda s: (s, 0, 0, 0))],
        out_specs=pl.BlockSpec((fields, 1, 2, rblock, nz), lambda s: (0, s, 0, 0, 0)),
        out_shape=jax.ShapeDtypeStruct((fields, nrad, 2, rblock, nz), F32),
    )(codes)


def per_device(forcing, diffusion, axial_forward, axial_inverse_map, axial_eigenvalues,
               radial_forward, radial_backward, radial_eigenvalues):
    fields, slab, rblock, nz = forcing.shape
    nm, nrad = lax.axis_size("modes"), lax.axis_size("rad")
    points, modes = slab * nm, nm * nrad
    cols = rblock * nz // nm
    halves = nz // cols
    bound = lax.pmax(jnp.max(jnp.abs(forcing)).astype(F32), ("modes", "rad"))
    bound = jnp.broadcast_to(jnp.maximum(bound, 1e-30), (8, cols))
    up, lo = azimuthal_tables(points, 2 * modes)
    x = forcing.reshape(fields, slab, rblock, halves, cols)
    x = x.transpose(2, 3, 0, 1, 4).reshape(nm, fields, slab, cols)
    got = lax.all_to_all(x, "modes", split_axis=0, concat_axis=0, tiled=True)
    codes = transform(up, lo, got, bound)
    codes = codes.reshape(fields, modes, 2, cols).transpose(1, 0, 2, 3)
    here = lax.all_to_all(codes, ("modes", "rad"), split_axis=0, concat_axis=0, tiled=True)
    here = here.transpose(1, 0, 2, 3).reshape(fields, 2 * modes, cols)
    back = solve(here, bound, diffusion, axial_forward, axial_inverse_map, axial_eigenvalues.reshape(1, nz),
                 radial_forward, radial_backward, radial_eigenvalues.reshape(-1, 1), rblock, nrad)
    back = lax.all_to_all(back, "rad", split_axis=0, concat_axis=0, tiled=True)
    return unpack(back, rblock)


def solution(mesh):
    in_specs = (P(None, "modes", "rad", None), P(), P(), P(), P(),
                P(("modes", "rad"), None, None), P(("modes", "rad"), None, None),
                P(("modes", "rad"), None))
    return jax.shard_map(per_device, mesh=mesh, in_specs=in_specs,
                         out_specs=P(None, "modes", None, "rad", None), check_vma=False)
```

time: 295 us -> 292 us (0.990); the launches traced: 291 us -> 292 us
  blocking collectives: 82.9 us -> 168 us
  waiting for transfers between devices: 97.9 us -> 44.4 us
  matrix products: 40.3 us -> 0 us
  Pallas kernels: 0 us -> 17.9 us
  starting transfers between devices: 34 us -> 28 us
  local copies, waits for them, and re-layouts: 17.7 us -> 13.7 us
    pmax x0 -> x1, blocking collectives: none -> 108 us  [per_device(): bound = lax.pmax(jnp.max(jnp.abs(forcing)).astype(F32), ('modes', 'rad'))]
    dot_general x6 -> x0, matrix products: 40.3 us -> none  [the longest x1 16.7 us: per_device(): jnp.dot(lo, got, preferred_element_type=jnp.float32)]
    all_to_all x1, waiting for transfers between devices: 77.6 us -> 44.4 us  [per_device(): lax.all_to_all(codes, ('modes', 'rad'), split_axis=0, concat_axis=0, tile...]
    all_to_all x1, blocking collectives: 82.9 us -> 60 us  [per_device(): back = lax.all_to_all(back, 'rad', split_axis=0, concat_axis=0, tiled=True)]
    all_to_all x1, waiting for transfers between devices: 20.4 us -> 0.01 us  [per_device(): got = lax.all_to_all(x, 'modes', split_axis=0, concat_axis=0, tiled=True)]
    pallas_call x0 -> x3, Pallas kernels: none -> 17.9 us  [the longest x1 8.31 us: solve(): pl.pallas_call(functools.partial(solve_kernel, rblock, nrad), grid=(field...]
    convert_element_type x1 -> x2, other arithmetic: 17.6 us -> 6.87 us  [the longest x1 4.37 us: azimuthal_tables(): lower = (table - lax.optimization_barrier(upper).astype(F32)).astype(BF16)]
    all_to_all x1, starting transfers between devices: 18.3 us -> 12.4 us  [per_device(): lax.all_to_all(codes, ('modes', 'rad'), split_axis=0, concat_axis=0, tile...]
  transfers between devices with their start and end apart: 2 -> 2, of which waited for: 2 -> 1; matrix products, arithmetic and copies ran while one was open for 6% -> 9% of each run, Pallas kernels for 0% -> 0%
where the time goes in v2:
time: 292 us
  blocking collectives  168 us (58%)
  waiting for transfers between devices  44.4 us (15%)
  starting transfers between devices  28 us (10%)
  other arithmetic  18.8 us (6%)
  Pallas kernels  17.9 us (6%)
  local copies, waits for them, and re-layouts  13.7 us (5%)
    pmax x1, blocking collectives, per_device(): bound = lax.pmax(jnp.max(jnp.abs(forcing)).astype(F32), ('modes', 'rad'))  108 us
    all_to_all x1, blocking collectives, per_device(): back = lax.all_to_all(back, 'rad', split_axis=0, concat_axis=0, tiled=True)  60 us
    all_to_all x1, waiting for transfers between devices, per_device(): lax.all_to_all(codes, ('modes', 'rad'), split_axis=0, concat_axis=0, tile...  44.4 us
    all_to_all x1, starting transfers between devices, per_device(): got = lax.all_to_all(x, 'modes', split_axis=0, concat_axis=0, tiled=True)  15.7 us
    all_to_all x1, starting transfers between devices, per_device(): lax.all_to_all(codes, ('modes', 'rad'), split_axis=0, concat_axis=0, tile...  12.4 us
    pallas_call x1, Pallas kernels, solve(): pl.pallas_call(functools.partial(solve_kernel, rblock, nrad), grid=(field...  8.31 us
    reshape x1, local copies, waits for them, and re-layouts, azimuthal_tables(): table = jnp.stack([real, imag], axis=2).reshape(rows, points)  6.06 us
  transfers between devices with their start and end apart: 2, of which 1 were waited for; matrix products, arithmetic and copies ran while one was open for 9% of the time, Pallas kernels for 0%

profile of v2, /device:TPU:32, one launch (start us, length us, event | category | flops | bytes accessed | tf_op | source)
XLA Modules:
  0.0 291.5 jit_solution(10951342125438717475)
XLA Ops:
  0.0 0.0 copy-start.7
  0.0 2.1 reshape.51
  2.1 1.8 copy.12
  3.9 15.7 %all-to-all-start = ((bf16[64,3,16,128]{3,2,1,0:T(8,128)(2,1)}), bf16[64,3,16,128]{3,2,1,0:T(8,128)(2,1)S(1)}, u32[]{:S(2)}, u32[]{:S(2)}) async-start(bf16[64,3,16,128]{3,2,1,0:T(8,128)(2,1)} %bitcast.1), calls=%async_computation | async-start | bytes 1572864 | tf_op jit(solution)/shard_map/all_to_all | solution.py:176
  19.6 0.0 copy-done.7
  19.6 0.7 abs_reduce_fusion
  20.3 108.1 %pmax.7 = f32[]{:T(128)} all-reduce(bf16[]{:T(256)} %abs_reduce_fusion), channel_id=1, replica_groups=mesh['modes'=64,'rad'=8] {'modes','rad'}, use_global_device_ids=true, to_apply=%region_1.0 | all-reduce | flops 1 | bytes 6 | tf_op jit(solution)/shard_map/pmax | solution.py:171
  128.4 0.5 sine_multiply_fusion
  128.9 0.3 fusion.12
  129.2 4.5 %multiply_subtract_fusion = (f32[16,32,1,1024]{3,2,1,0:T(1,128)S(1)}, f32[16,32,1,1024]{3,2,1,0:T(1,128)S(1)}) fusion(f32[32,1024]{1,0:T(8,128)S(1)} %get-tuple-element.12, f32[16,1024]{1,0:T(8,128)S(1)} %get-tuple-element.11, f32[32,1024]{1,0:T(8,128)S(1)} %get-tuple-element.10, f32[16,1024]{1,0:T(8,128)S(1)} %get-tuple-element.9), kind=kLoop, calls=%fused_computation.3 | loop fusion | flops 3670016 | bytes 4587520 | tf_op jit(solution)/shard_map/sub | solution.py:55
  133.7 5.8 %pad_maximum_fusion = f32[16,32,2,1024]{3,2,1,0:T(2,128)} fusion(f32[16,32,1,1024]{3,2,1,0:T(1,128)S(1)} %get-tuple-element.14, f32[16,32,1,1024]{3,2,1,0:T(1,128)S(1)} %get-tuple-element.13), kind=kLoop, calls=%fused_computation | loop fusion | flops 1048576 | bytes 8388608 | tf_op jit(solution)/shard_map/stack | solution.py:57
  139.5 6.1 %reshape.50 = f32[1024,1024]{1,0:T(8,128)} reshape(f32[16,32,2,1024]{3,2,1,0:T(2,128)} %pad_maximum_fusion) | data formatting | bytes 8388608 | tf_op jit(solution)/shard_map/reshape | solution.py:57
  145.6 2.5 convert_element_type.24.up_ref
  148.7 4.4 %subtract_convert_fusion.lo_ref = bf16[1024,1024]{1,0:T(8,128)(2,1)} fusion(f32[1024,1024]{1,0:T(8,128)} %reshape.50, bf16[1024,1024]{1,0:T(8,128)(2,1)S(1)} %convert_element_type.24.up_ref), kind=kLoop, calls=%fused_computation.1 | loop fusion | flops 3145728 | bytes 8388608 | tf_op jit(solution)/shard_map/convert_element_type | solution.py:59
  153.1 0.0 all-to-all-done.got_ref
  153.1 0.0 copy-start
  153.1 1.6 copy-done
  154.7 4.0 %shard_map.82 = bf16[3,1024,128]{2,1,0:T(8,128)(2,1)S(1)} custom-call(bf16[1024,1024]{1,0:T(8,128)(2,1)S(1)} %convert_element_type.24.up_ref, bf16[1024,1024]{1,0:T(8,128)(2,1)S(1)} %copy-done, bf16[64,3,16,128]{3,2,1,0:T(8,128)(2,1)S(1)} %all-to-all-done.got_ref, f32[8,128]{1,0:T(8,128)S(1)} %broadcast_in_dim.2.bound_ref), custom_call_target="tpu_custom_call" | custom-call | tf_op jit(solution)/shard_map/pallas_call | solution.py:78
  158.7 0.0 copy-start.8
  158.7 0.0 copy-start.1
  158.7 0.0 copy-start.2
  158.8 0.0 copy-start.3
  158.8 0.0 copy-start.4
  158.8 0.0 copy-start.5
  158.8 0.0 copy-start.6
  158.8 1.4 copy.17
  160.2 12.4 %all-to-all-start.1 = ((bf16[512,3,2,128]{3,2,1,0:T(2,128)(2,1)}), bf16[512,3,2,128]{3,2,1,0:T(2,128)(2,1)S(1)}, u32[]{:S(2)}, u32[]{:S(2)}) async-start(bf16[512,3,2,128]{3,2,1,0:T(2,128)(2,1)} %bitcast.12), calls=%async_computation.1 | async-start | bytes 1572864 | tf_op jit(solution)/shard_map/all_to_all | solution.py:179
  172.6 0.0 copy-done.8
  172.6 0.1 copy.15.reig_ref
  172.7 44.4 %all-to-all-done.1 = bf16[512,3,2,128]{3,2,1,0:T(2,128)(2,1)S(1)} async-done(((bf16[512,3,2,128]{3,2,1,0:T(2,128)(2,1)}), bf16[512,3,2,128]{3,2,1,0:T(2,128)(2,1)S(1)}, u32[]{:S(2)}, u32[]{:S(2)}) %all-to-all-start.1) | async-done | bytes 786464 | tf_op jit(solution)/shard_map/all_to_all | solution.py:179
  217.1 0.5 copy.14
  217.7 0.0 copy-done.1
  217.7 0.0 copy-done.2
  217.7 0.0 copy-done.3
  217.7 0.0 copy-done.4
  217.7 0.0 copy-done.5
  217.7 0.0 copy-done.6
  217.7 8.3 %shard_map.83 = bf16[8,3,80,256]{3,2,1,0:T(8,128)(2,1)S(1)} custom-call(bf16[3,1024,128]{2,1,0:T(8,128)(2,1)S(1)} %bitcast.14, f32[8,128]{1,0:T(8,128)S(1)} %broadcast_in_dim.2.bound_ref, f32[3]{0:T(128)S(1)} %copy-done.6, f32[256,256]{1,0:T(8,128)S(1)} %copy-done.1, f32[256,256]{1,0:T(8,128)S(1)} %copy-done.2, f32[1,256]{1,0:T(1,128)S(1)} %bitcast.15, ...), custom_call_target="tpu_custom_call" | custom-call | tf_op jit(solution)/shard_map/pallas_call | solution.py:133
  226.0 60.0 %all_to_all.15.codes_ref = bf16[8,3,80,256]{3,2,1,0:T(8,128)(2,1)} all-to-all(bf16[8,3,80,256]{3,2,1,0:T(8,128)(2,1)S(1)} %shard_map.83), channel_id=1, replica_groups=mesh['modes'=64,'rad'=8] {'rad'}, dimensions={0} | all-to-all | bytes 1966080 | tf_op jit(solution)/shard_map/all_to_all | solution.py:183
  286.0 5.5 %shard_map.84 = f32[3,8,2,32,256]{4,3,2,1,0:T(8,128)} custom-call(bf16[8,3,80,256]{3,2,1,0:T(8,128)(2,1)} %all_to_all.15.codes_ref), custom_call_target="tpu_custom_call" | custom-call | tf_op jit(solution)/shard_map/pallas_call | solution.py:155
  (2 shorter events, 0.0 us)
Async XLA Ops:
  0.0 19.6 %copy-start.7 = (bf16[3,16,32,256]{3,2,1,0:T(8,128)(2,1)S(1)}, bf16[3,16,32,256]{3,2,1,0:T(8,128)(2,1)}, u32[]{:S(2)}) copy-start(bf16[3,16,32,256]{3,2,1,0:T(8,128)(2,1)} %param.8) | copy-start | bytes 2359300
  3.9 149.2 %all-to-all-start = ((bf16[64,3,16,128]{3,2,1,0:T(8,128)(2,1)}), bf16[64,3,16,128]{3,2,1,0:T(8,128)(2,1)S(1)}, u32[]{:S(2)}, u32[]{:S(2)}) async-start(bf16[64,3,16,128]{3,2,1,0:T(8,128)(2,1)} %bitcast.1), calls=%async_computation | async-start | bytes 1572864 | tf_op jit(solution)/shard_map/all_to_all | solution.py:176
  153.1 1.6 copy-start
  158.7 13.9 %copy-start.8 = (f32[1,256]{1,0:T(1,128)S(1)}, f32[1,256]{1,0:T(1,128)}, u32[]{:S(2)}) copy-start(f32[1,256]{1,0:T(1,128)} %param.15) | copy-start | bytes 3076
  158.7 58.9 %copy-start.1 = (f32[256,256]{1,0:T(8,128)S(1)}, f32[256,256]{1,0:T(8,128)}, u32[]{:S(2)}) copy-start(f32[256,256]{1,0:T(8,128)} %af_ref.1) | copy-start | bytes 786436
  158.7 58.9 %copy-start.2 = (f32[256,256]{1,0:T(8,128)S(1)}, f32[256,256]{1,0:T(8,128)}, u32[]{:S(2)}) copy-start(f32[256,256]{1,0:T(8,128)} %ai_ref.1) | copy-start | bytes 786436
  158.8 58.9 %copy-start.3 = (f32[1,256,256]{2,1,0:T(8,128)S(1)}, f32[1,256,256]{2,1,0:T(8,128)}, u32[]{:S(2)}) copy-start(f32[1,256,256]{2,1,0:T(8,128)} %rf_ref.1) | copy-start | bytes 786436
  158.8 58.9 %copy-start.4 = (f32[1,256,256]{2,1,0:T(8,128)S(1)}, f32[1,256,256]{2,1,0:T(8,128)}, u32[]{:S(2)}) copy-start(f32[1,256,256]{2,1,0:T(8,128)} %rb_ref.1) | copy-start | bytes 786436
  158.8 58.9 %copy-start.5 = (f32[256]{0:T(256)S(1)}, f32[256]{0:T(256)}, u32[]{:S(2)}) copy-start(f32[256]{0:T(256)} %param.12) | copy-start | bytes 3076
  158.8 58.9 %copy-start.6 = (f32[3]{0:T(128)S(1)}, f32[3]{0:T(128)}, u32[]{:S(2)}) copy-start(f32[3]{0:T(128)} %diff_ref.1) | copy-start | bytes 40
  160.2 56.9 %all-to-all-start.1 = ((bf16[512,3,2,128]{3,2,1,0:T(2,128)(2,1)}), bf16[512,3,2,128]{3,2,1,0:T(2,128)(2,1)S(1)}, u32[]{:S(2)}, u32[]{:S(2)}) async-start(bf16[512,3,2,128]{3,2,1,0:T(2,128)(2,1)} %bitcast.12), calls=%async_computation.1 | async-start | bytes 1572864 | tf_op jit(solution)/shard_map/all_to_all | solution.py:179

commit v3 on v1

v3 whole, which is shorter than its diff:
```python
import functools
import math

import jax
import jax.numpy as jnp
from jax import lax
from jax.experimental import pallas as pl
from jax.experimental.pallas import tpu as pltpu
from jax.sharding import PartitionSpec as P

F32, BF16 = jnp.float32, jnp.bfloat16
MESH = pl.DeviceIdType.MESH
Z_LO, XS, CORES, Z_HI, YS = 8, 4, 2, 2, 4
SPECTRUM_OCTAVES, SOLVED_OCTAVES = 16, 10
TINY = 1e-30


def encode(x, inverse_floor, octaves):
    grown = jnp.log2(1.0 + jnp.abs(x) * inverse_floor)
    code = jnp.exp2(grown * (239.0 / octaves) - 120.0)
    return jnp.where(x < 0, -code, code).astype(BF16)


def decode(code, floor, octaves):
    code = code.astype(F32)
    grown = (jnp.log2(jnp.abs(code)) + 120.0) * (octaves / 239.0)
    size = (jnp.exp2(grown) - 1.0) * floor
    return jnp.where(code < 0, -size, size)


def split(x):
    high = x.astype(BF16)
    return high, (x - high.astype(F32)).astype(BF16)


def dot3(a, b, dims):
    d = functools.partial(lax.dot_general, dimension_numbers=(dims, ((), ())), preferred_element_type=F32)
    return d(a[0], b[0]) + (d(a[0], b[1]) + d(a[1], b[0]))


NN, NT_ = ((1,), (0,)), ((1,), (1,))


def mode_of(z, p):
    m = (z % Z_LO) * (XS * CORES) + p % (XS * CORES)
    return m * (Z_HI * YS) + (z // Z_LO) * YS + p // (XS * CORES)


def small_tables(points):
    t = jnp.arange(points, dtype=jnp.int32)
    turn = 2.0 * math.pi / points
    z = jnp.arange(Z_HI * Z_LO, dtype=jnp.int32)
    p = jnp.arange(YS * XS * CORES, dtype=jnp.int32)

    def angles(k):
        return ((k[:, None] * t[None, :]) % points).astype(F32) * turn

    coarse, fine = angles(mode_of(z, 0)), angles(mode_of(0, p))
    scale = 1.0 / math.sqrt(points)
    c, s = jnp.cos(fine) * scale, jnp.sin(fine) * scale
    rows = 2 * p.shape[0]
    first = jnp.stack([c, -s], axis=1).reshape(rows, points)
    second = jnp.stack([s, c], axis=1).reshape(rows, points)
    return jnp.cos(coarse), jnp.sin(coarse), first, second


def kernel(xs, cc, cs, f1, f2, diff, af, ai, qeig, rf, rb, reig, out,
           up, lo, r1, enc, r2, flat, s3, r3, x, s4, r4, mx1, mx1r, mx2, mx2r, sc, scr,
           t1_s, t1_r, mx_s, mx_r, z_s, z_r, xy_s, xy_r, t4_s, t4_r, sc_s, sc_r):
    me, rad = lax.axis_index("modes"), lax.axis_index("rad")
    fields, nm, slab, cols = xs.shape
    nrad, nz_, np_ = Z_HI * YS, Z_HI * Z_LO, YS * XS * CORES
    points = nm * slab
    rblock = XS * Z_LO
    nr, nz = rblock * nrad, CORES * cols
    inner = XS * CORES
    z, p = (rad // YS) * Z_LO + me // inner, (rad % YS) * inner + me % inner

    def at(zz, pp):
        return ((zz % Z_LO) * inner + pp % inner, (zz // Z_LO) * YS + pp // inner)

    def send(src, dst, s, r, to):
        pltpu.make_async_remote_copy(src_ref=src, dst_ref=dst, send_sem=s, recv_sem=r, device_id=to,
                                     device_id_type=MESH).start()

    def drain(ref, sem):
        pltpu.make_async_copy(ref, ref, sem).wait()

    barrier = pltpu.get_barrier_semaphore()

    @pl.loop(1, nm)
    def _(i):
        pl.semaphore_signal(barrier, inc=1, device_id=((me + i) % nm, rad), device_id_type=MESH)

    @pl.loop(1, nrad)
    def _(i):
        pl.semaphore_signal(barrier, inc=1, device_id=(me, (rad + i) % nrad), device_id_type=MESH)

    top = jnp.zeros((slab, cols), F32)
    for f in range(fields):
        top = jnp.maximum(top, jnp.max(jnp.abs(xs[f]).astype(F32), axis=0))
    top = jnp.max(jnp.max(top, axis=0, keepdims=True), axis=1, keepdims=True)
    mx1[...] = jnp.broadcast_to(top, (1, cols))
    pl.semaphore_wait(barrier, nm + nrad - 2)

    @pl.loop(1, nm)
    def _(i):
        m = (me + i) % nm
        send(mx1, mx1r.at[me], mx_s.at[0], mx_r.at[0], (m, rad))

    for f in range(fields):
        @pl.loop(1, nm)
        def _(i):
            m = (me + i) % nm
            send(xs.at[f, m], r1.at[f, me], t1_s.at[f], t1_r.at[f], (m, rad))

    mx1r[me] = mx1[...]
    for f in range(fields):
        r1[f, me] = xs[f, me]

    drain(mx1r.at[pl.ds(0, nm - 1)], mx_r.at[0])
    top = jnp.max(mx1r[...], axis=0)
    mx2[...] = top
    mx2r[rad] = top

    @pl.loop(1, nrad)
    def _(i):
        send(mx2, mx2r.at[rad], mx_s.at[1], mx_r.at[1], (me, (rad + i) % nrad))

    half = 2 * np_

    @pl.loop(0, nz_)
    def _(a):
        table = cc[pl.ds(a, 1), :] * f1[...] - cs[pl.ds(a, 1), :] * f2[...]
        high, low = split(table)
        rows = pl.ds(pl.multiple_of(a * half, half), half)
        up[rows, :] = high
        lo[rows, :] = low

    drain(mx2r.at[pl.ds(0, nrad - 1)], mx_r.at[1])
    bound = jnp.maximum(jnp.max(mx2r[...], axis=0), TINY)
    floor = bound * 2.0 ** (5 - SPECTRUM_OCTAVES)
    inverse_floor = 2.0 ** (SPECTRUM_OCTAVES - 5) / bound
    blocks = 4
    each = nz_ // blocks

    def transform(f):
        drain(r1.at[f, pl.ds(0, nm - 1)], t1_r.at[f])
        data = r1[f].reshape(points, cols)

        @pl.loop(0, blocks)
        def _(b):
            rows = pl.ds(pl.multiple_of(b * each * half, each * half), each * half)
            spec = jnp.dot(up[rows, :], data, preferred_element_type=F32) + jnp.dot(
                lo[rows, :], data, preferred_element_type=F32)
            enc[f, pl.ds(b * each, each)] = encode(spec, inverse_floor, SPECTRUM_OCTAVES).reshape(each, half, cols)

        @pl.loop(1, nz_)
        def _(i):
            to = (z + i) % nz_
            send(enc.at[f, to], r2.at[f, z], z_s.at[f], z_r.at[f], at(to, p))

        r2[f, z] = enc[f, z]

    def regroup(f):
        drain(r2.at[f, pl.ds(0, nz_ - 1)], z_r.at[f])
        flat[...] = r2[f].astype(F32).reshape(nz_ * half, cols)
        for q in range(np_):
            for c in range(2):
                s3[f, q, c * nz_:(c + 1) * nz_, :] = flat[pl.ds(2 * q + c, nz_, stride=half), :].astype(BF16)

        @pl.loop(1, np_)
        def _(i):
            to = (p + i) % np_
            send(s3.at[f, to], r3.at[f, p], xy_s.at[f], xy_r.at[f], at(z, to))

        r3[f, p] = s3[f, p]

    def solve(f):
        drain(r3.at[f, pl.ds(0, np_ - 1)], xy_r.at[f])
        for q in range(np_):
            y, xx, core = q // inner, (q // CORES) % XS, q % CORES
            value = decode(r3[f, q], floor, SPECTRUM_OCTAVES)
            for c in range(2):
                for h in range(Z_HI):
                    r0 = (h * YS + y) * rblock + xx * Z_LO
                    x[c, r0:r0 + Z_LO, core * cols:(core + 1) * cols] = value[
                        c * nz_ + h * Z_LO:c * nz_ + (h + 1) * Z_LO]
        axial = dot3(split(x[...].reshape(2 * nr, nz)), split(af[...]), NT_)
        denominator = 1.0 + diff[f] * (reig[...] + qeig[...])
        result = []
        for c in range(2):
            scaled = dot3(split(rf[0]), split(axial[c * nr:(c + 1) * nr]), NN) / denominator
            result.append(dot3(split(dot3(split(rb[0]), split(scaled), NN)), split(ai[...]), NT_))
        top = jnp.maximum(jnp.max(jnp.abs(result[0]), axis=0, keepdims=True),
                          jnp.max(jnp.abs(result[1]), axis=0, keepdims=True))
        top = jnp.maximum(jnp.broadcast_to(jnp.max(top, axis=1, keepdims=True), (1, nz)), TINY)
        sc[f] = top
        scr[f, rad] = top
        inverse = 2.0 ** SOLVED_OCTAVES / top
        for c in range(2):
            code = encode(result[c], inverse, SOLVED_OCTAVES)
            for s in range(nrad):
                s4[f, s, c] = code[s * rblock:(s + 1) * rblock]

        @pl.loop(1, nrad)
        def _(i):
            to = (rad + i) % nrad
            send(sc.at[f], scr.at[f, rad], sc_s.at[f], sc_r.at[f], (me, to))
            send(s4.at[f, to], r4.at[f, rad], t4_s.at[f], t4_r.at[f], (me, to))

        r4[f, rad] = s4[f, rad]

    def unpack(f):
        drain(scr.at[f, pl.ds(0, nrad - 1)], sc_r.at[f])
        drain(r4.at[f, pl.ds(0, nrad - 1)], t4_r.at[f])

        @pl.loop(0, nrad)
        def _(s):
            low = scr[f, s] * 2.0 ** -SOLVED_OCTAVES
            for c in range(2):
                out[f, s, c] = decode(r4[f, s, c], low, SOLVED_OCTAVES)

    transform(0)
    transform(1)
    regroup(0)
    transform(2)
    regroup(1)
    solve(0)
    regroup(2)
    solve(1)
    solve(2)
    for f in range(fields):
        unpack(f)

    drain(mx1r.at[pl.ds(0, nm - 1)], mx_s.at[0])
    drain(mx2r.at[pl.ds(0, nrad - 1)], mx_s.at[1])
    for f in range(fields):
        drain(r1.at[f, pl.ds(0, nm - 1)], t1_s.at[f])
        drain(r2.at[f, pl.ds(0, nz_ - 1)], z_s.at[f])
        drain(r3.at[f, pl.ds(0, np_ - 1)], xy_s.at[f])
        drain(scr.at[f, pl.ds(0, nrad - 1)], sc_s.at[f])
        drain(r4.at[f, pl.ds(0, nrad - 1)], t4_s.at[f])


def per_device(forcing, diffusion, axial_forward, axial_inverse_map, axial_eigenvalues,
               radial_forward, radial_backward, radial_eigenvalues):
    fields, slab, rblock, nz = forcing.shape
    nm, nrad = lax.axis_size("modes"), lax.axis_size("rad")
    points, cols = slab * nm, nz // CORES
    nzs, nps = Z_HI * Z_LO, YS * XS * CORES
    xs = forcing.reshape(fields, slab, XS, Z_LO, CORES, cols).transpose(0, 3, 2, 4, 1, 5)
    xs = xs.reshape(fields, nm, slab, cols)
    tables = small_tables(points)
    dma = pltpu.SemaphoreType.DMA
    vmem = pl.BlockSpec(memory_space=pltpu.VMEM)
    args = (xs, *tables, diffusion, axial_forward, axial_inverse_map, axial_eigenvalues.reshape(1, nz),
            radial_forward, radial_backward, radial_eigenvalues.reshape(-1, 1))
    specs = [vmem] * len(args)
    specs[5] = pl.BlockSpec(memory_space=pltpu.SMEM)
    return pl.pallas_call(
        kernel,
        out_shape=jax.ShapeDtypeStruct((fields, nrad, 2, rblock, nz), F32),
        in_specs=specs,
        out_specs=vmem,
        scratch_shapes=[
            pltpu.VMEM((2 * nzs * nps, points), BF16), pltpu.VMEM((2 * nzs * nps, points), BF16),
            pltpu.VMEM((fields, nm, slab, cols), BF16),
            pltpu.VMEM((fields, nzs, 2 * nps, cols), BF16), pltpu.VMEM((fields, nzs, 2 * nps, cols), BF16),
            pltpu.VMEM((nzs * 2 * nps, cols), F32),
            pltpu.VMEM((fields, nps, 2 * nzs, cols), BF16), pltpu.VMEM((fields, nps, 2 * nzs, cols), BF16),
            pltpu.VMEM((2, rblock * nrad, nz), F32),
            pltpu.VMEM((fields, nrad, 2, rblock, nz), BF16), pltpu.VMEM((fields, nrad, 2, rblock, nz), BF16),
            pltpu.VMEM((1, cols), F32), pltpu.VMEM((nm, 1, cols), F32),
            pltpu.VMEM((1, cols), F32), pltpu.VMEM((nrad, 1, cols), F32),
            pltpu.VMEM((fields, 1, nz), F32), pltpu.VMEM((fields, nrad, 1, nz), F32),
            dma((fields,)), dma((fields,)), dma((2,)), dma((2,)), dma((fields,)), dma((fields,)),
            dma((fields,)), dma((fields,)), dma((fields,)), dma((fields,)), dma((fields,)), dma((fields,)),
        ],
        compiler_params=pltpu.CompilerParams(collective_id=0, has_side_effects=True, vmem_limit_bytes=56 << 20),
    )(*args)


def solution(mesh):
    in_specs = (P(None, "modes", "rad", None), P(), P(), P(), P(),
                P(("modes", "rad"), None, None), P(("modes", "rad"), None, None),
                P(("modes", "rad"), None))
    return jax.shard_map(per_device, mesh=mesh, in_specs=in_specs,
                         out_specs=P(None, "modes", None, "rad", None), check_vma=False)
```

time: 295 us -> 161 us (0.55)
  the two profiles are of different devices: /device:TPU:32 before, /device:TPU:24 now
where the time goes in v3:
time: 161 us
  Pallas kernels  152 us (94%)
  local copies, waits for them, and re-layouts  7.77 us (5%)
  other arithmetic  1.66 us (1%)
    pallas_call x1, Pallas kernels, per_device(): pl.pallas_call(kernel, out_shape=jax.ShapeDtypeStruct((fields, nrad, 2, r...  152 us

profile of v3, /device:TPU:24, one launch (start us, length us, event | category | flops | bytes accessed | tf_op | source)
XLA Modules:
  0.0 161.1 jit_solution(87175531387857251)
XLA Ops:
  0.0 1.0 fusion.13
  1.0 1.5 copy.15.reig
  2.5 0.6 sine_multiply_fusion
  3.1 0.0 copy-start
  3.1 0.2 copy.14
  3.4 0.9 reshape.189.f2
  4.2 0.2 copy.13
  4.4 0.9 reshape.188.f1
  5.3 0.0 copy-done
  5.3 1.4 copy.12
  6.7 151.7 %shard_map.82 = f32[3,8,2,32,256]{4,3,2,1,0:T(8,128)} custom-call(bf16[3,64,16,128]{3,2,1,0:T(8,128)(2,1)} %bitcast.6, f32[16,1024]{1,0:T(8,128)} %get-tuple-element.11.cc, f32[16,1024]{1,0:T(8,128)} %get-tuple-element.10.cs, f32[64,1024]{1,0:T(8,128)} %reshape.188.f1, f32[64,1024]{1,0:T(8,128)} %reshape.189.f2, f32[3]{0:T(128)} %diff.1, f32[256,256]{1,0:T(8,128)} %af.1, ...), custom_call_target="tpu_custom_call" | custom-call | tf_op jit(solution)/shard_map/pallas_call | solution.py:261
  158.4 2.7 %copy.17 = f32[3,8,2,32,256]{4,3,2,1,0:T(8,128)} copy(f32[3,8,2,32,256]{4,3,2,1,0:T(8,128)} %shard_map.82) | data formatting | bytes 3145728
  (3 shorter events, 0.1 us)
Async XLA Ops:
  3.1 2.3 %copy-start = (bf16[3,16,32,256]{3,2,1,0:T(8,128)(2,1)S(1)}, bf16[3,16,32,256]{3,2,1,0:T(8,128)(2,1)}, u32[]{:S(2)}) copy-start(bf16[3,16,32,256]{3,2,1,0:T(8,128)(2,1)} %param.8) | copy-start | bytes 2359300

commit v4 on v3

--- a/solution.py
+++ b/solution.py
@@ -3,6 +3,7 @@
 
 import jax
 import jax.numpy as jnp
+import numpy as np
 from jax import lax
 from jax.experimental import pallas as pl
 from jax.experimental.pallas import tpu as pltpu
@@ -47,26 +48,15 @@
 
 
 def small_tables(points):
-    t = jnp.arange(points, dtype=jnp.int32)
-    turn = 2.0 * math.pi / points
-    z = jnp.arange(Z_HI * Z_LO, dtype=jnp.int32)
-    p = jnp.arange(YS * XS * CORES, dtype=jnp.int32)
-
-    def angles(k):
-        return ((k[:, None] * t[None, :]) % points).astype(F32) * turn
-
-    coarse, fine = angles(mode_of(z, 0)), angles(mode_of(0, p))
-    scale = 1.0 / math.sqrt(points)
-    c, s = jnp.cos(fine) * scale, jnp.sin(fine) * scale
-    rows = 2 * p.shape[0]
-    first = jnp.stack([c, -s], axis=1).reshape(rows, points)
-    second = jnp.stack([s, c], axis=1).reshape(rows, points)
-    return jnp.cos(coarse), jnp.sin(coarse), first, second
-
-
-def kernel(xs, cc, cs, f1, f2, diff, af, ai, qeig, rf, rb, reig, out,
+    k = [mode_of(z, 0) for z in range(Z_HI * Z_LO)] + [mode_of(0, p) for p in range(YS * XS * CORES)]
+    turns = np.outer(np.array(k), np.arange(points)) % points
+    radians = turns * (2.0 * math.pi / points)
+    return np.cos(radians).astype(np.float32), np.sin(radians).astype(np.float32)
+
+
+def kernel(forcing, cosine, sine, diff, af, ai, qeig, rf, rb, reig, out,
            up, lo, r1, enc, r2, flat, s3, r3, x, s4, r4, mx1, mx1r, mx2, mx2r, sc, scr,
-           t1_s, t1_r, mx_s, mx_r, z_s, z_r, xy_s, xy_r, t4_s, t4_r, sc_s, sc_r):
+           t1_s, t1_r, mx_s, mx_r, z_s, z_r, xy_s, xy_r, t4_s, t4_r, sc_s, sc_r, rp, rp_s, rp_r, fw_s, eigen, xs, wide, ob, out_s):
     me, rad = lax.axis_index("modes"), lax.axis_index("rad")
     fields, nm, slab, cols = xs.shape
     nrad, nz_, np_ = Z_HI * YS, Z_HI * Z_LO, YS * XS * CORES
@@ -96,24 +86,38 @@
     def _(i):
         pl.semaphore_signal(barrier, inc=1, device_id=(me, (rad + i) % nrad), device_id_type=MESH)
 
+    def spread(f):
+        for core in range(CORES):
+            wide[core] = forcing[f, :, :, core * cols:(core + 1) * cols].astype(F32).reshape(slab * rblock, cols)
+        for m in range(nm):
+            row = m // CORES % XS * Z_LO + m // inner
+            xs[f, m] = wide[m % CORES, pl.ds(row, slab, stride=rblock), :].astype(BF16)
+
+    def begin(f):
+        @pl.loop(1, nm)
+        def _(i):
+            m = (me + i) % nm
+            send(xs.at[f, m], r1.at[f, me], t1_s.at[f], t1_r.at[f], (m, rad))
+
+    spread(0)
+    pl.semaphore_wait(barrier, nm + nrad - 2)
+    begin(0)
     top = jnp.zeros((slab, cols), F32)
     for f in range(fields):
-        top = jnp.maximum(top, jnp.max(jnp.abs(xs[f]).astype(F32), axis=0))
+        for core in range(CORES):
+            top = jnp.maximum(top, jnp.max(
+                jnp.abs(forcing[f, :, :, core * cols:(core + 1) * cols].astype(F32)), axis=1))
     top = jnp.max(jnp.max(top, axis=0, keepdims=True), axis=1, keepdims=True)
     mx1[...] = jnp.broadcast_to(top, (1, cols))
-    pl.semaphore_wait(barrier, nm + nrad - 2)
 
     @pl.loop(1, nm)
     def _(i):
         m = (me + i) % nm
         send(mx1, mx1r.at[me], mx_s.at[0], mx_r.at[0], (m, rad))
 
-    for f in range(fields):
-        @pl.loop(1, nm)
-        def _(i):
-            m = (me + i) % nm
-            send(xs.at[f, m], r1.at[f, me], t1_s.at[f], t1_r.at[f], (m, rad))
-
+    for f in range(1, fields):
+        spread(f)
+        begin(f)
     mx1r[me] = mx1[...]
     for f in range(fields):
         r1[f, me] = xs[f, me]
@@ -127,15 +131,18 @@
     def _(i):
         send(mx2, mx2r.at[rad], mx_s.at[1], mx_r.at[1], (me, (rad + i) % nrad))
 
-    half = 2 * np_
+    half, hop, scale = 2 * np_, nz_ // 4, 1.0 / math.sqrt(points)
+    eigen[...] = jnp.transpose(jnp.broadcast_to(reig[...], (nz, nr))) + qeig[...]
 
     @pl.loop(0, nz_)
     def _(a):
-        table = cc[pl.ds(a, 1), :] * f1[...] - cs[pl.ds(a, 1), :] * f2[...]
-        high, low = split(table)
-        rows = pl.ds(pl.multiple_of(a * half, half), half)
-        up[rows, :] = high
-        lo[rows, :] = low
+        ca, sa = cosine[pl.ds(a, 1), :] * scale, sine[pl.ds(a, 1), :] * scale
+        cb, sb = cosine[nz_:, :], sine[nz_:, :]
+        for c, table in enumerate((ca * cb - sa * sb, -(sa * cb + ca * sb))):
+            high, low = split(table)
+            rows = pl.ds(pl.multiple_of(a * half + c * np_, np_), np_)
+            up[rows, :] = high
+            lo[rows, :] = low
 
     drain(mx2r.at[pl.ds(0, nrad - 1)], mx_r.at[1])
     bound = jnp.maximum(jnp.max(mx2r[...], axis=0), TINY)
@@ -167,7 +174,7 @@
         flat[...] = r2[f].astype(F32).reshape(nz_ * half, cols)
         for q in range(np_):
             for c in range(2):
-                s3[f, q, c * nz_:(c + 1) * nz_, :] = flat[pl.ds(2 * q + c, nz_, stride=half), :].astype(BF16)
+                s3[f, q, c * nz_:(c + 1) * nz_, :] = flat[pl.ds(c * np_ + q, nz_, stride=half), :].astype(BF16)
 
         @pl.loop(1, np_)
         def _(i):
@@ -187,7 +194,7 @@
                     x[c, r0:r0 + Z_LO, core * cols:(core + 1) * cols] = value[
                         c * nz_ + h * Z_LO:c * nz_ + (h + 1) * Z_LO]
         axial = dot3(split(x[...].reshape(2 * nr, nz)), split(af[...]), NT_)
-        denominator = 1.0 + diff[f] * (reig[...] + qeig[...])
+        denominator = 1.0 + diff[f] * eigen[...]
         result = []
         for c in range(2):
             scaled = dot3(split(rf[0]), split(axial[c * nr:(c + 1) * nr]), NN) / denominator
@@ -203,13 +210,31 @@
             for s in range(nrad):
                 s4[f, s, c] = code[s * rblock:(s + 1) * rblock]
 
+        far = (1 - rad // YS) * YS
+
+        @pl.loop(0, YS)
+        def _(y):
+            send(s4.at[f, far + y, 0], rp.at[f, 0, rad % YS], rp_s.at[f], rp_r.at[f, 0],
+                 at((z + hop) % nz_, y * inner + p % inner))
+            send(s4.at[f, far + y, 1], rp.at[f, 1, rad % YS], rp_s.at[f], rp_r.at[f, 1],
+                 at((z + nz_ - hop) % nz_, y * inner + p % inner))
+
+        @pl.loop(1, YS)
+        def _(i):
+            to = rad // YS * YS + (rad + i) % YS
+            send(s4.at[f, to], r4.at[f, rad], t4_s.at[f], t4_r.at[f], (me, to))
+
         @pl.loop(1, nrad)
         def _(i):
-            to = (rad + i) % nrad
-            send(sc.at[f], scr.at[f, rad], sc_s.at[f], sc_r.at[f], (me, to))
-            send(s4.at[f, to], r4.at[f, rad], t4_s.at[f], t4_r.at[f], (me, to))
+            send(sc.at[f], scr.at[f, rad], sc_s.at[f], sc_r.at[f], (me, (rad + i) % nrad))
 
         r4[f, rad] = s4[f, rad]
+
+    def relay(f):
+        for part, step in ((0, hop), (1, nz_ - hop)):
+            drain(rp.at[f, part], rp_r.at[f, part])
+            source = (z + nz_ - step) % nz_ // Z_LO * YS
+            send(rp.at[f, part], r4.at[f, pl.ds(source, YS), part], fw_s.at[f], t4_r.at[f], at((z + step) % nz_, p))
 
     def unpack(f):
         drain(scr.at[f, pl.ds(0, nrad - 1)], sc_r.at[f])
@@ -219,7 +244,9 @@
         def _(s):
             low = scr[f, s] * 2.0 ** -SOLVED_OCTAVES
             for c in range(2):
-                out[f, s, c] = decode(r4[f, s, c], low, SOLVED_OCTAVES)
+                ob[f, s, c] = decode(r4[f, s, c], low, SOLVED_OCTAVES)
+
+        pltpu.make_async_copy(ob.at[f], out.at[f], out_s.at[f]).start()
 
     transform(0)
     transform(1)
@@ -229,9 +256,15 @@
     solve(0)
     regroup(2)
     solve(1)
+    relay(0)
     solve(2)
+    relay(1)
+    unpack(0)
+    relay(2)
+    unpack(1)
+    unpack(2)
     for f in range(fields):
-        unpack(f)
+        pltpu.make_async_copy(ob.at[f], out.at[f], out_s.at[f]).wait()
 
     drain(mx1r.at[pl.ds(0, nm - 1)], mx_s.at[0])
     drain(mx2r.at[pl.ds(0, nrad - 1)], mx_s.at[1])
@@ -240,7 +273,9 @@
         drain(r2.at[f, pl.ds(0, nz_ - 1)], z_s.at[f])
         drain(r3.at[f, pl.ds(0, np_ - 1)], xy_s.at[f])
         drain(scr.at[f, pl.ds(0, nrad - 1)], sc_s.at[f])
-        drain(r4.at[f, pl.ds(0, nrad - 1)], t4_s.at[f])
+        drain(r4.at[f, pl.ds(0, YS - 1)], t4_s.at[f])
+        drain(r4.at[f, pl.ds(0, YS)], rp_s.at[f])
+        drain(r4.at[f, pl.ds(0, YS)], fw_s.at[f])
 
 
 def per_device(forcing, diffusion, axial_forward, axial_inverse_map, axial_eigenvalues,
@@ -249,20 +284,18 @@
     nm, nrad = lax.axis_size("modes"), lax.axis_size("rad")
     points, cols = slab * nm, nz // CORES
     nzs, nps = Z_HI * Z_LO, YS * XS * CORES
-    xs = forcing.reshape(fields, slab, XS, Z_LO, CORES, cols).transpose(0, 3, 2, 4, 1, 5)
-    xs = xs.reshape(fields, nm, slab, cols)
-    tables = small_tables(points)
+    tables = [jnp.asarray(t) for t in small_tables(points)]
     dma = pltpu.SemaphoreType.DMA
     vmem = pl.BlockSpec(memory_space=pltpu.VMEM)
-    args = (xs, *tables, diffusion, axial_forward, axial_inverse_map, axial_eigenvalues.reshape(1, nz),
-            radial_forward, radial_backward, radial_eigenvalues.reshape(-1, 1))
+    args = (forcing, *tables, diffusion, axial_forward, axial_inverse_map, axial_eigenvalues.reshape(1, nz),
+            radial_forward, radial_backward, radial_eigenvalues)
     specs = [vmem] * len(args)
-    specs[5] = pl.BlockSpec(memory_space=pltpu.SMEM)
+    specs[3] = pl.BlockSpec(memory_space=pltpu.SMEM)
     return pl.pallas_call(
         kernel,
         out_shape=jax.ShapeDtypeStruct((fields, nrad, 2, rblock, nz), F32),
         in_specs=specs,
-        out_specs=vmem,
+        out_specs=pl.BlockSpec(memory_space=pl.ANY),
         scratch_shapes=[
             pltpu.VMEM((2 * nzs * nps, points), BF16), pltpu.VMEM((2 * nzs * nps, points), BF16),
             pltpu.VMEM((fields, nm, slab, cols), BF16),
@@ -276,6 +309,9 @@
             pltpu.VMEM((fields, 1, nz), F32), pltpu.VMEM((fields, nrad, 1, nz), F32),
             dma((fields,)), dma((fields,)), dma((2,)), dma((2,)), dma((fields,)), dma((fields,)),
             dma((fields,)), dma((fields,)), dma((fields,)), dma((fields,)), dma((fields,)), dma((fields,)),
+            pltpu.VMEM((fields, 2, YS, rblock, nz), BF16), dma((fields,)), dma((fields, 2)), dma((fields,)),
+            pltpu.VMEM((rblock * nrad, nz), F32), pltpu.VMEM((fields, nm, slab, cols), BF16),
+            pltpu.VMEM((CORES, slab * rblock, cols), F32), pltpu.VMEM((fields, nrad, 2, rblock, nz), F32), dma((fields,)),
         ],
         compiler_params=pltpu.CompilerParams(collective_id=0, has_side_effects=True, vmem_limit_bytes=56 << 20),
     )(*args)

time: 161 us -> 139 us (0.86)
  the two profiles are of different devices: /device:TPU:24 before, /device:TPU:58 now
where the time goes in v4:
time: 139 us
  Pallas kernels  136 us (98%)
  local copies, waits for them, and re-layouts  2.73 us (2%)
    pallas_call x1, Pallas kernels, per_device(): pl.pallas_call(kernel, out_shape=jax.ShapeDtypeStruct((fields, nrad, 2, r...  136 us

profile of v4, /device:TPU:58, one launch (start us, length us, event | category | flops | bytes accessed | tf_op | source)
XLA Modules:
  0.0 138.9 jit_solution(12754678239190789790)
XLA Ops:
  0.0 136.2 %shard_map.100 = f32[3,8,2,32,256]{4,3,2,1,0:T(8,128)} custom-call(bf16[3,16,32,256]{3,2,1,0:T(8,128)(2,1)} %forcing.1, f32[48,1024]{1,0:T(8,128)} %constant.4.clone.cosine, f32[48,1024]{1,0:T(8,128)} %constant.5.clone.sine, f32[3]{0:T(128)} %diff.1, f32[256,256]{1,0:T(8,128)} %af.1, f32[256,256]{1,0:T(8,128)} %ai.1, f32[1,256]{1,0:T(1,128)} %bitcast.1, ...), custom_call_target="tpu_custom_call" | custom-call | tf_op jit(solution)/shard_map/pallas_call | solution.py:294
  136.2 2.7 %copy.12 = f32[3,8,2,32,256]{4,3,2,1,0:T(8,128)} copy(f32[3,8,2,32,256]{4,3,2,1,0:T(8,128)} %shard_map.100) | data formatting | bytes 3145728

commit v5 on v4

--- a/solution.py
+++ b/solution.py
@@ -54,9 +54,10 @@
     return np.cos(radians).astype(np.float32), np.sin(radians).astype(np.float32)
 
 
-def kernel(forcing, cosine, sine, diff, af, ai, qeig, rf, rb, reig, out,
+def kernel(forcing_, cosine_, sine_, diff_, af_, ai_, qeig_, rf_, rb_, reig_, out,
            up, lo, r1, enc, r2, flat, s3, r3, x, s4, r4, mx1, mx1r, mx2, mx2r, sc, scr,
-           t1_s, t1_r, mx_s, mx_r, z_s, z_r, xy_s, xy_r, t4_s, t4_r, sc_s, sc_r, rp, rp_s, rp_r, fw_s, eigen, xs, wide, ob, out_s):
+           t1_s, t1_r, mx_s, mx_r, z_s, z_r, xy_s, xy_r, t4_s, t4_r, sc_s, sc_r, rp, rp_s, rp_r, fw_s, eigen, xs, wide,
+           forcing, cosine, sine, diff, af, ai, qeig, rf, rb, reig, in_s):
     me, rad = lax.axis_index("modes"), lax.axis_index("rad")
     fields, nm, slab, cols = xs.shape
     nrad, nz_, np_ = Z_HI * YS, Z_HI * Z_LO, YS * XS * CORES
@@ -76,6 +77,12 @@
     def drain(ref, sem):
         pltpu.make_async_copy(ref, ref, sem).wait()
 
+    loads = [pltpu.make_async_copy(forcing_, forcing, in_s.at[0])]
+    for n, (src, dst) in enumerate(((cosine_, cosine), (sine_, sine), (diff_, diff), (af_, af), (ai_, ai), (qeig_, qeig), (rf_, rf),
+                                  (rb_, rb), (reig_, reig))):
+        loads.append(pltpu.make_async_copy(src, dst, in_s.at[n + 1]))
+    for load in loads:
+        load.start()
     barrier = pltpu.get_barrier_semaphore()
 
     @pl.loop(1, nm)
@@ -99,9 +106,7 @@
             m = (me + i) % nm
             send(xs.at[f, m], r1.at[f, me], t1_s.at[f], t1_r.at[f], (m, rad))
 
-    spread(0)
-    pl.semaphore_wait(barrier, nm + nrad - 2)
-    begin(0)
+    loads[0].wait()
     top = jnp.zeros((slab, cols), F32)
     for f in range(fields):
         for core in range(CORES):
@@ -109,19 +114,16 @@
                 jnp.abs(forcing[f, :, :, core * cols:(core + 1) * cols].astype(F32)), axis=1))
     top = jnp.max(jnp.max(top, axis=0, keepdims=True), axis=1, keepdims=True)
     mx1[...] = jnp.broadcast_to(top, (1, cols))
+    spread(0)
+    pl.semaphore_wait(barrier, nm + nrad - 2)
 
     @pl.loop(1, nm)
     def _(i):
-        m = (me + i) % nm
-        send(mx1, mx1r.at[me], mx_s.at[0], mx_r.at[0], (m, rad))
-
-    for f in range(1, fields):
-        spread(f)
-        begin(f)
+        send(mx1, mx1r.at[me], mx_s.at[0], mx_r.at[0], ((me + i) % nm, rad))
+
+    begin(0)
     mx1r[me] = mx1[...]
-    for f in range(fields):
-        r1[f, me] = xs[f, me]
-
+    spread(1)
     drain(mx1r.at[pl.ds(0, nm - 1)], mx_r.at[0])
     top = jnp.max(mx1r[...], axis=0)
     mx2[...] = top
@@ -131,6 +133,14 @@
     def _(i):
         send(mx2, mx2r.at[rad], mx_s.at[1], mx_r.at[1], (me, (rad + i) % nrad))
 
+    begin(1)
+    spread(2)
+    begin(2)
+    for f in range(fields):
+        r1[f, me] = xs[f, me]
+
+    for load in loads[1:]:
+        load.wait()
     half, hop, scale = 2 * np_, nz_ // 4, 1.0 / math.sqrt(points)
     eigen[...] = jnp.transpose(jnp.broadcast_to(reig[...], (nz, nr))) + qeig[...]
 
@@ -161,13 +171,11 @@
             spec = jnp.dot(up[rows, :], data, preferred_element_type=F32) + jnp.dot(
                 lo[rows, :], data, preferred_element_type=F32)
             enc[f, pl.ds(b * each, each)] = encode(spec, inverse_floor, SPECTRUM_OCTAVES).reshape(each, half, cols)
-
-        @pl.loop(1, nz_)
-        def _(i):
-            to = (z + i) % nz_
-            send(enc.at[f, to], r2.at[f, z], z_s.at[f], z_r.at[f], at(to, p))
-
         r2[f, z] = enc[f, z]
+
+    def send_z(f, i):
+        to = (z + i) % nz_
+        send(enc.at[f, to], r2.at[f, z], z_s.at[f], z_r.at[f], at(to, p))
 
     def regroup(f):
         drain(r2.at[f, pl.ds(0, nz_ - 1)], z_r.at[f])
@@ -175,13 +183,11 @@
         for q in range(np_):
             for c in range(2):
                 s3[f, q, c * nz_:(c + 1) * nz_, :] = flat[pl.ds(c * np_ + q, nz_, stride=half), :].astype(BF16)
-
-        @pl.loop(1, np_)
-        def _(i):
-            to = (p + i) % np_
-            send(s3.at[f, to], r3.at[f, p], xy_s.at[f], xy_r.at[f], at(z, to))
-
         r3[f, p] = s3[f, p]
+
+    def send_xy(f, i):
+        to = (p + i) % np_
+        send(s3.at[f, to], r3.at[f, p], xy_s.at[f], xy_r.at[f], at(z, to))
 
     def solve(f):
         drain(r3.at[f, pl.ds(0, np_ - 1)], xy_r.at[f])
@@ -194,7 +200,7 @@
                     x[c, r0:r0 + Z_LO, core * cols:(core + 1) * cols] = value[
                         c * nz_ + h * Z_LO:c * nz_ + (h + 1) * Z_LO]
         axial = dot3(split(x[...].reshape(2 * nr, nz)), split(af[...]), NT_)
-        denominator = 1.0 + diff[f] * eigen[...]
+        denominator = 1.0 + diff[0:1, f:f + 1] * eigen[...]
         result = []
         for c in range(2):
             scaled = dot3(split(rf[0]), split(axial[c * nr:(c + 1) * nr]), NN) / denominator
@@ -210,25 +216,25 @@
             for s in range(nrad):
                 s4[f, s, c] = code[s * rblock:(s + 1) * rblock]
 
-        far = (1 - rad // YS) * YS
-
-        @pl.loop(0, YS)
-        def _(y):
-            send(s4.at[f, far + y, 0], rp.at[f, 0, rad % YS], rp_s.at[f], rp_r.at[f, 0],
-                 at((z + hop) % nz_, y * inner + p % inner))
-            send(s4.at[f, far + y, 1], rp.at[f, 1, rad % YS], rp_s.at[f], rp_r.at[f, 1],
-                 at((z + nz_ - hop) % nz_, y * inner + p % inner))
+        r4[f, rad] = s4[f, rad]
+
+    far = (1 - rad // YS) * YS
+
+    def send_far(f, y):
+        send(s4.at[f, far + y, 0], rp.at[f, 0, rad % YS], rp_s.at[f], rp_r.at[f, 0],
+             at((z + hop) % nz_, y * inner + p % inner))
+        send(s4.at[f, far + y, 1], rp.at[f, 1, rad % YS], rp_s.at[f], rp_r.at[f, 1],
+             at((z + nz_ - hop) % nz_, y * inner + p % inner))
+
+    def send_near(f):
+        @pl.loop(1, nrad)
+        def _(i):
+            send(sc.at[f], scr.at[f, rad], sc_s.at[f], sc_r.at[f], (me, (rad + i) % nrad))
 
         @pl.loop(1, YS)
         def _(i):
             to = rad // YS * YS + (rad + i) % YS
             send(s4.at[f, to], r4.at[f, rad], t4_s.at[f], t4_r.at[f], (me, to))
-
-        @pl.loop(1, nrad)
-        def _(i):
-            send(sc.at[f], scr.at[f, rad], sc_s.at[f], sc_r.at[f], (me, (rad + i) % nrad))
-
-        r4[f, rad] = s4[f, rad]
 
     def relay(f):
         for part, step in ((0, hop), (1, nz_ - hop)):
@@ -244,27 +250,61 @@
         def _(s):
             low = scr[f, s] * 2.0 ** -SOLVED_OCTAVES
             for c in range(2):
-                ob[f, s, c] = decode(r4[f, s, c], low, SOLVED_OCTAVES)
-
-        pltpu.make_async_copy(ob.at[f], out.at[f], out_s.at[f]).start()
+                out[f, s, c] = decode(r4[f, s, c], low, SOLVED_OCTAVES)
+
+    def mixed(f, start, stop, g):
+        per = np_ // (stop - start)
+
+        @pl.loop(start, stop)
+        def _(i):
+            @pl.when(i > 0)
+            def _():
+                send_z(f, i)
+
+            for j in range(per):
+                k = (i - start) * per + j
+
+                @pl.when(k > 0)
+                def _():
+                    send_xy(g, k)
 
     transform(0)
+    pl.loop(1, nz_)(functools.partial(send_z, 0))
     transform(1)
+    pl.loop(1, nz_)(functools.partial(send_z, 1))
+    transform(2)
     regroup(0)
-    transform(2)
+    mixed(2, 0, nz_ // 2, 0)
     regroup(1)
+    mixed(2, nz_ // 2, nz_, 1)
     solve(0)
+    pl.loop(0, YS // 2)(functools.partial(send_far, 0))
     regroup(2)
+
+    @pl.loop(YS // 2, YS)
+    def _(y):
+        send_far(0, y)
+        per = np_ // (YS - YS // 2)
+        for j in range(per):
+            k = (y - YS // 2) * per + j
+
+            @pl.when(k > 0)
+            def _():
+                send_xy(2, k)
+
+    send_near(0)
     solve(1)
+    pl.loop(0, YS)(functools.partial(send_far, 1))
+    send_near(1)
     relay(0)
     solve(2)
+    pl.loop(0, YS)(functools.partial(send_far, 2))
+    send_near(2)
     relay(1)
     unpack(0)
     relay(2)
     unpack(1)
     unpack(2)
-    for f in range(fields):
-        pltpu.make_async_copy(ob.at[f], out.at[f], out_s.at[f]).wait()
 
     drain(mx1r.at[pl.ds(0, nm - 1)], mx_s.at[0])
     drain(mx2r.at[pl.ds(0, nrad - 1)], mx_s.at[1])
@@ -287,15 +327,15 @@
     tables = [jnp.asarray(t) for t in small_tables(points)]
     dma = pltpu.SemaphoreType.DMA
     vmem = pl.BlockSpec(memory_space=pltpu.VMEM)
-    args = (forcing, *tables, diffusion, axial_forward, axial_inverse_map, axial_eigenvalues.reshape(1, nz),
+    args = (forcing, *tables, diffusion.reshape(1, fields), axial_forward, axial_inverse_map, axial_eigenvalues.reshape(1, nz),
             radial_forward, radial_backward, radial_eigenvalues)
-    specs = [vmem] * len(args)
-    specs[3] = pl.BlockSpec(memory_space=pltpu.SMEM)
+    args = [pltpu.with_memory_space_constraint(a, pltpu.HBM) for a in args]
+    specs = [pl.BlockSpec(memory_space=pltpu.HBM)] * len(args)
     return pl.pallas_call(
         kernel,
         out_shape=jax.ShapeDtypeStruct((fields, nrad, 2, rblock, nz), F32),
         in_specs=specs,
-        out_specs=pl.BlockSpec(memory_space=pl.ANY),
+        out_specs=vmem,
         scratch_shapes=[
             pltpu.VMEM((2 * nzs * nps, points), BF16), pltpu.VMEM((2 * nzs * nps, points), BF16),
             pltpu.VMEM((fields, nm, slab, cols), BF16),
@@ -311,9 +351,10 @@
             dma((fields,)), dma((fields,)), dma((fields,)), dma((fields,)), dma((fields,)), dma((fields,)),
             pltpu.VMEM((fields, 2, YS, rblock, nz), BF16), dma((fields,)), dma((fields, 2)), dma((fields,)),
             pltpu.VMEM((rblock * nrad, nz), F32), pltpu.VMEM((fields, nm, slab, cols), BF16),
-            pltpu.VMEM((CORES, slab * rblock, cols), F32), pltpu.VMEM((fields, nrad, 2, rblock, nz), F32), dma((fields,)),
+            pltpu.VMEM((CORES, slab * rblock, cols), F32),
+            *(pltpu.VMEM(a.shape, a.dtype) for a in args), dma((len(args),)),
         ],
-        compiler_params=pltpu.CompilerParams(collective_id=0, has_side_effects=True, vmem_limit_bytes=56 << 20),
+        compiler_params=pltpu.CompilerParams(collective_id=0, has_side_effects=True, vmem_limit_bytes=48 << 20),
     )(*args)
 
 

time: 139 us -> 135 us (0.971)
  the two profiles are of different devices: /device:TPU:58 before, /device:TPU:26 now
where the time goes in v5:
time: 135 us
  Pallas kernels  134 us (99%)
    pallas_call x1, Pallas kernels, per_device(): pl.pallas_call(kernel, out_shape=jax.ShapeDtypeStruct((fields, nrad, 2, r...  134 us

profile of v5, /device:TPU:26, one launch (start us, length us, event | category | flops | bytes accessed | tf_op | source)
XLA Modules:
  0.0 134.8 jit_solution(13253666178686722380)
XLA Ops:
  0.0 133.7 %shard_map.100 = f32[3,8,2,32,256]{4,3,2,1,0:T(8,128)S(1)} custom-call(bf16[3,16,32,256]{3,2,1,0:T(8,128)(2,1)} %forcing_.1, f32[48,1024]{1,0:T(8,128)} %constant.4.clone.cosine_, f32[48,1024]{1,0:T(8,128)} %constant.5.clone.sine_, f32[1,3]{1,0:T(1,128)} %bitcast.3, f32[256,256]{1,0:T(8,128)} %af_.1, f32[256,256]{1,0:T(8,128)} %ai_.1, f32[1,256]{1,0:T(1,128)} %bitcast.2, ...), custom_call_target="tpu_custom_call" | custom-call | tf_op jit(solution)/shard_map/pallas_call | solution.py:334
  133.7 1.1 copy.12

commit v6 on v5

--- a/solution.py
+++ b/solution.py
@@ -56,7 +56,7 @@
 
 def kernel(forcing_, cosine_, sine_, diff_, af_, ai_, qeig_, rf_, rb_, reig_, out,
            up, lo, r1, enc, r2, flat, s3, r3, x, s4, r4, mx1, mx1r, mx2, mx2r, sc, scr,
-           t1_s, t1_r, mx_s, mx_r, z_s, z_r, xy_s, xy_r, t4_s, t4_r, sc_s, sc_r, rp, rp_s, rp_r, fw_s, eigen, xs, wide,
+           t1_s, t1_r, mx_s, mx_r, z_s, z_r, xy_s, xy_r, t4_s, t4_r, sc_s, sc_r, rp, rp_s, rp_r, fw_s, fw_r, eigen, xs, wide,
            forcing, cosine, sine, diff, af, ai, qeig, rf, rb, reig, in_s):
     me, rad = lax.axis_index("modes"), lax.axis_index("rad")
     fields, nm, slab, cols = xs.shape
@@ -81,8 +81,7 @@
     for n, (src, dst) in enumerate(((cosine_, cosine), (sine_, sine), (diff_, diff), (af_, af), (ai_, ai), (qeig_, qeig), (rf_, rf),
                                   (rb_, rb), (reig_, reig))):
         loads.append(pltpu.make_async_copy(src, dst, in_s.at[n + 1]))
-    for load in loads:
-        load.start()
+    loads[0].start()
     barrier = pltpu.get_barrier_semaphore()
 
     @pl.loop(1, nm)
@@ -106,7 +105,12 @@
             m = (me + i) % nm
             send(xs.at[f, m], r1.at[f, me], t1_s.at[f], t1_r.at[f], (m, rad))
 
+    for load in loads[1:]:
+        load.start()
     loads[0].wait()
+    spread(0)
+    pl.semaphore_wait(barrier, nm + nrad - 2)
+    begin(0)
     top = jnp.zeros((slab, cols), F32)
     for f in range(fields):
         for core in range(CORES):
@@ -114,16 +118,15 @@
                 jnp.abs(forcing[f, :, :, core * cols:(core + 1) * cols].astype(F32)), axis=1))
     top = jnp.max(jnp.max(top, axis=0, keepdims=True), axis=1, keepdims=True)
     mx1[...] = jnp.broadcast_to(top, (1, cols))
-    spread(0)
-    pl.semaphore_wait(barrier, nm + nrad - 2)
 
     @pl.loop(1, nm)
     def _(i):
         send(mx1, mx1r.at[me], mx_s.at[0], mx_r.at[0], ((me + i) % nm, rad))
 
-    begin(0)
     mx1r[me] = mx1[...]
     spread(1)
+    begin(1)
+    spread(2)
     drain(mx1r.at[pl.ds(0, nm - 1)], mx_r.at[0])
     top = jnp.max(mx1r[...], axis=0)
     mx2[...] = top
@@ -133,8 +136,6 @@
     def _(i):
         send(mx2, mx2r.at[rad], mx_s.at[1], mx_r.at[1], (me, (rad + i) % nrad))
 
-    begin(1)
-    spread(2)
     begin(2)
     for f in range(fields):
         r1[f, me] = xs[f, me]
@@ -240,17 +241,20 @@
         for part, step in ((0, hop), (1, nz_ - hop)):
             drain(rp.at[f, part], rp_r.at[f, part])
             source = (z + nz_ - step) % nz_ // Z_LO * YS
-            send(rp.at[f, part], r4.at[f, pl.ds(source, YS), part], fw_s.at[f], t4_r.at[f], at((z + step) % nz_, p))
+            send(rp.at[f, part], r4.at[f, pl.ds(source, YS), part], fw_s.at[f], fw_r.at[f], at((z + step) % nz_, p))
 
     def unpack(f):
         drain(scr.at[f, pl.ds(0, nrad - 1)], sc_r.at[f])
-        drain(r4.at[f, pl.ds(0, nrad - 1)], t4_r.at[f])
-
-        @pl.loop(0, nrad)
-        def _(s):
+
+        def widen(s):
             low = scr[f, s] * 2.0 ** -SOLVED_OCTAVES
             for c in range(2):
                 out[f, s, c] = decode(r4[f, s, c], low, SOLVED_OCTAVES)
+
+        drain(r4.at[f, pl.ds(0, YS - 1)], t4_r.at[f])
+        pl.loop(rad // YS * YS, rad // YS * YS + YS)(widen)
+        drain(r4.at[f, pl.ds(0, YS)], fw_r.at[f])
+        pl.loop(far, far + YS)(widen)
 
     def mixed(f, start, stop, g):
         per = np_ // (stop - start)
@@ -349,7 +353,7 @@
             pltpu.VMEM((fields, 1, nz), F32), pltpu.VMEM((fields, nrad, 1, nz), F32),
             dma((fields,)), dma((fields,)), dma((2,)), dma((2,)), dma((fields,)), dma((fields,)),
             dma((fields,)), dma((fields,)), dma((fields,)), dma((fields,)), dma((fields,)), dma((fields,)),
-            pltpu.VMEM((fields, 2, YS, rblock, nz), BF16), dma((fields,)), dma((fields, 2)), dma((fields,)),
+            pltpu.VMEM((fields, 2, YS, rblock, nz), BF16), dma((fields,)), dma((fields, 2)), dma((fields,)), dma((fields,)),
             pltpu.VMEM((rblock * nrad, nz), F32), pltpu.VMEM((fields, nm, slab, cols), BF16),
             pltpu.VMEM((CORES, slab * rblock, cols), F32),
             *(pltpu.VMEM(a.shape, a.dtype) for a in args), dma((len(args),)),

time: 135 us -> 133 us (0.985)
  the two profiles are of different devices: /device:TPU:26 before, /device:TPU:52 now
where the time goes in v6:
time: 133 us
  Pallas kernels  132 us (99%)
    pallas_call x1, Pallas kernels, per_device(): pl.pallas_call(kernel, out_shape=jax.ShapeDtypeStruct((fields, nrad, 2, r...  132 us

profile of v6, /device:TPU:52, one launch (start us, length us, event | category | flops | bytes accessed | tf_op | source)
XLA Modules:
  0.0 133.0 jit_solution(16015644752134668824)
XLA Ops:
  0.0 131.8 %shard_map.100 = f32[3,8,2,32,256]{4,3,2,1,0:T(8,128)S(1)} custom-call(bf16[3,16,32,256]{3,2,1,0:T(8,128)(2,1)} %forcing_.1, f32[48,1024]{1,0:T(8,128)} %constant.4.clone.cosine_, f32[48,1024]{1,0:T(8,128)} %constant.5.clone.sine_, f32[1,3]{1,0:T(1,128)} %bitcast.3, f32[256,256]{1,0:T(8,128)} %af_.1, f32[256,256]{1,0:T(8,128)} %ai_.1, f32[1,256]{1,0:T(1,128)} %bitcast.2, ...), custom_call_target="tpu_custom_call" | custom-call | tf_op jit(solution)/shard_map/pallas_call | solution.py:338
  131.8 1.1 copy.12
